TPU v7x, 32 devices: a whole 2x2x4 slice. The times are simulated.
32 devices in a mesh: row: 2 (over x), col: 16 (over z, y, core).
Axes of the slice: x: 2, y: 2, z: 4, core: 2. Of those that a mesh axis runs over, the one named last changes fastest.
Arguments:
- trace_maps: bfloat16 [2, 16, 1280, 1280], P('row', 'col'), may hold values from -0.125 to 0.125
- sources: bfloat16 [2, 16, 1280, 256], P('row', 'col'), may hold values from -6 to 6
Outputs:
- traces: bfloat16 [2, 16, 1280, 256], P('row', 'col')
All inputs are finite; a program needn't handle non-finite values.
Results may differ from a plain program's by a relative error of at most 0.007.
Values may be sent and summed in bfloat16 or wider, within the bound.
No kernel may reach another device: no remote copies, remote signals or barrier semaphores. Data moves between devices by JAX's collectives and lax.ppermute only.
A program may use at most 64 MiB of HBM per device.

v0:
```python
import functools

import jax
import jax.numpy as jnp
from jax import lax
from jax.experimental import pallas as pl
from jax.experimental.pallas import tpu as pltpu
from jax.sharding import PartitionSpec as P


ITERS = 8
LAG = 1

LIMIT = 12 * 1024 * 1024
COST = pl.CostEstimate(flops=400_000_000, bytes_accessed=2_000_000, transcendentals=0)
VMEM = pl.BlockSpec(memory_space=pltpu.VMEM)


def in_vmem(array):
    return pltpu.with_memory_space_constraint(array, pltpu.VMEM)


def call(body, outs, *operands):
    operands = [in_vmem(operand) for operand in operands]
    return pl.pallas_call(
            body,
            out_shape=[pltpu.VMEM(*(out if isinstance(out[0], tuple) else (out, jnp.bfloat16))) for out in outs],
            in_specs=[VMEM] * len(operands),
            out_specs=[VMEM] * len(outs),
            compiler_params=pltpu.CompilerParams(vmem_limit_bytes=LIMIT),
            cost_estimate=COST,
    )(*operands)


def dot(left, right):
    return jnp.dot(left, right, preferred_element_type=jnp.float32)


def load_body(mapping, source, map_own, source_own, sems):
    copies = [
        pltpu.make_async_copy(source, source_own, sems.at[0]),
        pltpu.make_async_copy(mapping, map_own, sems.at[1]),
    ]
    for copy in copies:
        copy.start()
    for copy in copies:
        copy.wait()


def load(mapping, source):
    return pl.pallas_call(
        load_body,
        out_shape=[pltpu.VMEM(array.shape, array.dtype) for array in (mapping, source)],
        in_specs=[pl.BlockSpec(memory_space=pltpu.HBM)] * 2,
        out_specs=[VMEM] * 2,
        scratch_shapes=[pltpu.SemaphoreType.DMA((2,))],
        compiler_params=pltpu.CompilerParams(vmem_limit_bytes=LIMIT),
        cost_estimate=COST,
        name="load",
    )(*[pltpu.with_memory_space_constraint(array, pltpu.HBM) for array in (mapping, source)])


def pick_body(own, got, source_a, source_b, right_a, upper_a, right_b, upper_b):
    half, width = right_a.shape
    core = lax.rem(lax.axis_index("col"), 2)
    for k in range(2):
        @pl.when(core == k)
        def _():
            first, second = (own, got) if k == 0 else (got, own)
            part = slice(k * width, (k + 1) * width)
            source_a[...] = first[:, part]
            source_b[...] = second[:, part]
            right_a[...] = first[:half, part]
            upper_a[...] = first[half:, part]
            right_b[...] = second[:half, part]
            upper_b[...] = second[half:, part]


def sort_body(own, got, map_a, map_b):
    core = lax.rem(lax.axis_index("col"), 2)

    def copy(k, first, second):
        @pl.when(core == k)
        def _():
            @pl.loop(0, first.shape[0] // 128)
            def _(i):
                rows = pl.ds(pl.multiple_of(i * 128, 128), 128)
                map_a[rows, :] = first[rows, :]
                map_b[rows, :] = second[rows, :]

    copy(0, own, got)
    copy(1, got, own)


def incoming(first, right_in):
    if not first:
        return right_in[...]
    return jnp.where(lax.axis_index("col") < 2, jnp.zeros_like(right_in), right_in[...])


def step_body(first, slot, rows, mapping, right_in, upper_in, source, old_right, old_upper, right, upper):
    half = right.shape[0]
    row = lax.axis_index("row")
    time = slot - LAG * row
    active = jnp.logical_and(time >= 0, time < ITERS - 1)

    @pl.when(jnp.logical_and(active, row == 0))
    def _():
        total = dot(mapping[:, :half], incoming(first, right_in)) + source[...].astype(jnp.float32)
        right[...] = total[:half].astype(right.dtype)
        upper[...] = total[half:].astype(upper.dtype)

    @pl.when(jnp.logical_and(active, jnp.logical_and(row > 0, row == rows - 1)))
    def _():
        total = dot(mapping[:half, :half], incoming(first, right_in)) + dot(mapping[:half, half:], upper_in[...])
        right[...] = (total + source[:half, :].astype(jnp.float32)).astype(right.dtype)
        upper[...] = old_upper[...]

    if rows > 2:
        @pl.when(jnp.logical_and(active, jnp.logical_and(row > 0, row < rows - 1)))
        def _():
            total = dot(mapping[:, :half], incoming(first, right_in)) + dot(mapping[:, half:], upper_in[...])
            total = total + source[...].astype(jnp.float32)
            right[...] = total[:half].astype(right.dtype)
            upper[...] = total[half:].astype(upper.dtype)

    @pl.when(jnp.logical_not(active))
    def _():
        right[...] = old_right[...]
        upper[...] = old_upper[...]


def give_body(first, second, sent):
    core = lax.rem(lax.axis_index("col"), 2)

    @pl.when(core == 0)
    def _():
        sent[...] = first[...]

    @pl.when(core == 1)
    def _():
        sent[...] = second[...]


def join_body(first, second, got, whole):
    width = got.shape[1]
    core = lax.rem(lax.axis_index("col"), 2)

    @pl.when(core == 0)
    def _():
        whole[:, :width] = first[...]
        whole[:, width:] = got[...]

    @pl.when(core == 1)
    def _():
        whole[:, :width] = got[...]
        whole[:, width:] = second[...]


def begin_body(mapping, right_in, source, total):
    half = right_in.shape[0]
    left = jnp.where(lax.axis_index("col") == 0, jnp.zeros_like(right_in), right_in[...])
    total[...] = dot(mapping[:, :half], left) + source[...].astype(jnp.float32)


def last_body(mapping, total, upper_in, out, ready, sems):
    half = upper_in.shape[0]
    parts = sems.shape[0]
    tall = total.shape[0] // parts
    copies = []
    below = jnp.where(lax.axis_index("row") == 0, jnp.zeros_like(upper_in), upper_in[...])
    for n in range(parts):
        rows = slice(n * tall, (n + 1) * tall)
        ready[rows, :] = (total[rows, :] + dot(mapping[rows, half:], below)).astype(ready.dtype)
        copy = pltpu.make_async_copy(ready.at[rows, :], out.at[rows, :], sems.at[n])
        copy.start()
        copies.append(copy)
    for copy in copies:
        copy.wait()


def last(mapping, total, upper_in, shape):
    operands = [in_vmem(operand) for operand in (mapping, total, upper_in)]
    return pl.pallas_call(
        last_body,
        out_shape=jax.ShapeDtypeStruct(shape, jnp.bfloat16),
        in_specs=[VMEM] * 3,
        out_specs=pl.BlockSpec(memory_space=pltpu.HBM),
        scratch_shapes=[pltpu.VMEM(shape, jnp.bfloat16), pltpu.SemaphoreType.DMA((2,))],
        compiler_params=pltpu.CompilerParams(vmem_limit_bytes=LIMIT),
        cost_estimate=COST,
        name="last",
    )(*operands)


def relax(trace_maps, sources):
    mapping = trace_maps[0, 0]
    source = sources[0, 0]
    order, width = source.shape
    half, part = order // 2, width // 2
    rows = lax.axis_size("row")
    count = lax.axis_size("col")
    swap = [(j, j ^ 1) for j in range(count)]
    cross = [(j, (j + 2) % count) for j in range(count)]
    up = [(i, (i + 1) % rows) for i in range(rows)]
    slots = ITERS - 1 + LAG * (rows - 1)
    last_message = ITERS - 2 + LAG * (rows - 2)

    def exchange(array):
        return lax.ppermute(array, "col", swap)

    def rightward(array):
        return lax.ppermute(array, "col", cross)

    def upward(array):
        return lax.ppermute(array, "row", up)

    source_got = exchange(source)
    map_got = exchange(mapping)
    map_own, source_own = load(mapping, source)
    trace, state = (half, part), (order, part)
    source_a, source_b, right_a, upper_a, right_b, upper_b = call(
        pick_body, [state] * 2 + [trace] * 4, source_own, source_got)
    below_b = [upward(upper_b)]
    left = rightward(right_b)
    below_a = [upward(upper_a)]
    map_a, map_b = call(sort_body, [(order, order)] * 2, map_own, map_got)

    def advance(column, slot, *operands):
        body = functools.partial(step_body, column == "a", slot, rows)
        return call(body, [trace] * 2, *operands)

    zero = jnp.zeros(trace, jnp.bfloat16)
    for slot in range(slots):
        message = slot - 1 - LAG
        in_b = below_b[message + 1] if message >= -1 else zero
        in_a = below_a[message + 1] if message >= -1 else zero
        new_right_b, upper_b = advance("b", slot, map_b, right_a, in_b, source_b, right_b, upper_b)
        new_left = rightward(new_right_b)
        if slot < last_message:
            below_b.append(upward(upper_b))
        right_a, upper_a = advance("a", slot, map_a, left, in_a, source_a, right_a, upper_a)
        if slot < last_message:
            below_a.append(upward(upper_a))
        elif slot == last_message:
            given, = call(give_body, [trace], upper_b, upper_a)
            whole, = call(join_body, [(half, width)], upper_a, upper_b, exchange(given))
            below_last = upward(whole)
        right_b, left = new_right_b, new_left

    given, = call(give_body, [trace], right_a, left)
    right_in, = call(join_body, [(half, width)], left, right_a, exchange(given))
    total, = call(begin_body, [((order, width), jnp.float32)], map_own, right_in, source_own)
    out = last(map_own, total, below_last, (order, width))
    return out[None, None]


def solution(mesh):
    placed = (P("row", "col", None, None), P("row", "col", None, None))

    return jax.shard_map(
        relax,
        mesh=mesh,
        in_specs=placed,
        out_specs=P("row", "col", None, None),
        check_vma=False,
    )
```

profile of v0, /device:TPU:0, one launch (start us, length us, event | category | flops | bytes accessed | tf_op | source)
XLA Modules:
  0.0 74.6 jit_solution(18313522313576718063)
XLA Ops:
  0.5 2.2 %load.1 = (bf16[1280,1280]{1,0:T(8,128)(2,1)S(1)}, bf16[1280,256]{1,0:T(8,128)(2,1)S(1)}) custom-call(bf16[1280,1280]{1,0:T(8,128)(2,1)} %bitcast.4, bf16[1280,256]{1,0:T(8,128)(2,1)} %bitcast.6), custom_call_target="tpu_custom_call" | custom-call | flops 400000000 | bytes 2000000 | tf_op jit(solution)/shard_map/load/pallas_call | solution.py:51
  2.7 4.4 %collective-permute-done.1.got = bf16[1280,256]{1,0:T(8,128)(2,1)S(1)} collective-permute-done((bf16[1280,256]{1,0:T(8,128)(2,1)}, bf16[1280,256]{1,0:T(8,128)(2,1)S(1)}, u32[]{:S(2)}, u32[]{:S(2)}) %collective-permute-start.1) | collective-permute-done | bytes 655392 | tf_op jit(solution)/shard_map/ppermute | solution.py:210
  7.3 2.9 %collective-permute-start.2 = (bf16[640,128]{1,0:T(8,128)(2,1)S(1)}, bf16[640,128]{1,0:T(8,128)(2,1)S(1)}, u32[]{:S(2)}, u32[]{:S(2)}) collective-permute-start(bf16[640,128]{1,0:T(8,128)(2,1)S(1)} %get-tuple-element.49.old_right), channel_id=1, source_target_pairs={{0,2},{1,3},{2,4},{3,5},{4,6},{5,7},{6,8},{7,9},{8,10},{9,11},{10,... | collective-permute-start | bytes 491528 | tf_op jit(solution)/shard_map/ppermute | solution.py:213
  10.3 1.5 %collective-permute-start.3 = (bf16[640,128]{1,0:T(8,128)(2,1)S(1)}, bf16[640,128]{1,0:T(8,128)(2,1)S(1)}, u32[]{:S(2)}, u32[]{:S(2)}) collective-permute-start(bf16[640,128]{1,0:T(8,128)(2,1)S(1)} %get-tuple-element.54.old_upper), channel_id=1, source_target_pairs={{0,16},{16,0},{1,17},{17,1},{2,18},{18,2},{3,19},{19,3},{4,20},{20... | collective-permute-start | bytes 491528 | tf_op jit(solution)/shard_map/ppermute | solution.py:216
  13.4 1.6 %collective-permute-start.6 = (bf16[640,128]{1,0:T(8,128)(2,1)S(1)}, bf16[640,128]{1,0:T(8,128)(2,1)S(1)}, u32[]{:S(2)}, u32[]{:S(2)}) collective-permute-start(bf16[640,128]{1,0:T(8,128)(2,1)S(1)} %get-tuple-element.56.old_right), channel_id=1, source_target_pairs={{0,2},{1,3},{2,4},{3,5},{4,6},{5,7},{6,8},{7,9},{8,10},{9,11},{10,... | collective-permute-start | bytes 491528 | tf_op jit(solution)/shard_map/ppermute | solution.py:213
  15.9 1.9 %collective-permute-done.2.right_in = bf16[640,128]{1,0:T(8,128)(2,1)S(1)} collective-permute-done((bf16[640,128]{1,0:T(8,128)(2,1)S(1)}, bf16[640,128]{1,0:T(8,128)(2,1)S(1)}, u32[]{:S(2)}, u32[]{:S(2)}) %collective-permute-start.2) | collective-permute-done | bytes 163872 | tf_op jit(solution)/shard_map/ppermute | solution.py:213
  25.0 1.6 %collective-permute-start.12 = (bf16[640,128]{1,0:T(8,128)(2,1)S(1)}, bf16[640,128]{1,0:T(8,128)(2,1)S(1)}, u32[]{:S(2)}, u32[]{:S(2)}) collective-permute-start(bf16[640,128]{1,0:T(8,128)(2,1)S(1)} %get-tuple-element.64.old_right), channel_id=1, source_target_pairs={{0,2},{1,3},{2,4},{3,5},{4,6},{5,7},{6,8},{7,9},{8,10},{9,11},{10,... | collective-permute-start | bytes 491528 | tf_op jit(solution)/shard_map/ppermute | solution.py:213
  26.5 1.5 %collective-permute-start.13 = (bf16[640,128]{1,0:T(8,128)(2,1)S(1)}, bf16[640,128]{1,0:T(8,128)(2,1)S(1)}, u32[]{:S(2)}, u32[]{:S(2)}) collective-permute-start(bf16[640,128]{1,0:T(8,128)(2,1)S(1)} %get-tuple-element.61.old_upper), channel_id=1, source_target_pairs={{0,16},{16,0},{1,17},{17,1},{2,18},{18,2},{3,19},{19,3},{4,20},{20... | collective-permute-start | bytes 491528 | tf_op jit(solution)/shard_map/ppermute | solution.py:216
  29.2 2.2 %collective-permute-done.8.upper_in = bf16[640,128]{1,0:T(8,128)(2,1)S(1)} collective-permute-done((bf16[640,128]{1,0:T(8,128)(2,1)S(1)}, bf16[640,128]{1,0:T(8,128)(2,1)S(1)}, u32[]{:S(2)}, u32[]{:S(2)}) %collective-permute-start.8) | collective-permute-done | bytes 163872 | tf_op jit(solution)/shard_map/ppermute | solution.py:216
  32.0 1.6 %collective-permute-start.10 = (bf16[640,128]{1,0:T(8,128)(2,1)S(1)}, bf16[640,128]{1,0:T(8,128)(2,1)S(1)}, u32[]{:S(2)}, u32[]{:S(2)}) collective-permute-start(bf16[640,128]{1,0:T(8,128)(2,1)S(1)} %get-tuple-element.66.old_right), channel_id=1, source_target_pairs={{0,2},{1,3},{2,4},{3,5},{4,6},{5,7},{6,8},{7,9},{8,10},{9,11},{10,... | collective-permute-start | bytes 491528 | tf_op jit(solution)/shard_map/ppermute | solution.py:213
  36.2 2.2 %collective-permute-done.15.upper_in = bf16[640,128]{1,0:T(8,128)(2,1)S(1)} collective-permute-done((bf16[640,128]{1,0:T(8,128)(2,1)S(1)}, bf16[640,128]{1,0:T(8,128)(2,1)S(1)}, u32[]{:S(2)}, u32[]{:S(2)}) %collective-permute-start.15) | collective-permute-done | bytes 163872 | tf_op jit(solution)/shard_map/ppermute | solution.py:216
  39.0 1.6 %collective-permute-start.18 = (bf16[640,128]{1,0:T(8,128)(2,1)S(1)}, bf16[640,128]{1,0:T(8,128)(2,1)S(1)}, u32[]{:S(2)}, u32[]{:S(2)}) collective-permute-start(bf16[640,128]{1,0:T(8,128)(2,1)S(1)} %get-tuple-element.72.old_right), channel_id=1, source_target_pairs={{0,2},{1,3},{2,4},{3,5},{4,6},{5,7},{6,8},{7,9},{8,10},{9,11},{10,... | collective-permute-start | bytes 491528 | tf_op jit(solution)/shard_map/ppermute | solution.py:213
  40.6 1.5 %collective-permute-start.19 = (bf16[640,128]{1,0:T(8,128)(2,1)S(1)}, bf16[640,128]{1,0:T(8,128)(2,1)S(1)}, u32[]{:S(2)}, u32[]{:S(2)}) collective-permute-start(bf16[640,128]{1,0:T(8,128)(2,1)S(1)} %get-tuple-element.69.old_upper), channel_id=1, source_target_pairs={{0,16},{16,0},{1,17},{17,1},{2,18},{18,2},{3,19},{19,3},{4,20},{20... | collective-permute-start | bytes 491528 | tf_op jit(solution)/shard_map/ppermute | solution.py:216
  43.4 2.0 %collective-permute-done.14.upper_in = bf16[640,128]{1,0:T(8,128)(2,1)S(1)} collective-permute-done((bf16[640,128]{1,0:T(8,128)(2,1)S(1)}, bf16[640,128]{1,0:T(8,128)(2,1)S(1)}, u32[]{:S(2)}, u32[]{:S(2)}) %collective-permute-start.14) | collective-permute-done | bytes 163872 | tf_op jit(solution)/shard_map/ppermute | solution.py:216
  46.0 1.6 %collective-permute-start.16 = (bf16[640,128]{1,0:T(8,128)(2,1)S(1)}, bf16[640,128]{1,0:T(8,128)(2,1)S(1)}, u32[]{:S(2)}, u32[]{:S(2)}) collective-permute-start(bf16[640,128]{1,0:T(8,128)(2,1)S(1)} %get-tuple-element.74.old_right), channel_id=1, source_target_pairs={{0,2},{1,3},{2,4},{3,5},{4,6},{5,7},{6,8},{7,9},{8,10},{9,11},{10,... | collective-permute-start | bytes 491528 | tf_op jit(solution)/shard_map/ppermute | solution.py:213
  47.6 1.5 %collective-permute-start.17 = (bf16[640,128]{1,0:T(8,128)(2,1)S(1)}, bf16[640,128]{1,0:T(8,128)(2,1)S(1)}, u32[]{:S(2)}, u32[]{:S(2)}) collective-permute-start(bf16[640,128]{1,0:T(8,128)(2,1)S(1)} %get-tuple-element.75.old_upper), channel_id=1, source_target_pairs={{0,16},{16,0},{1,17},{17,1},{2,18},{18,2},{3,19},{19,3},{4,20},{20... | collective-permute-start | bytes 491528 | tf_op jit(solution)/shard_map/ppermute | solution.py:216
  50.3 2.2 %collective-permute-done.21.upper_in = bf16[640,128]{1,0:T(8,128)(2,1)S(1)} collective-permute-done((bf16[640,128]{1,0:T(8,128)(2,1)S(1)}, bf16[640,128]{1,0:T(8,128)(2,1)S(1)}, u32[]{:S(2)}, u32[]{:S(2)}) %collective-permute-start.21) | collective-permute-done | bytes 163872 | tf_op jit(solution)/shard_map/ppermute | solution.py:216
  54.1 1.9 %collective-permute-done.17.upper_in = bf16[640,128]{1,0:T(8,128)(2,1)S(1)} collective-permute-done((bf16[640,128]{1,0:T(8,128)(2,1)S(1)}, bf16[640,128]{1,0:T(8,128)(2,1)S(1)}, u32[]{:S(2)}, u32[]{:S(2)}) %collective-permute-start.17) | collective-permute-done | bytes 163872 | tf_op jit(solution)/shard_map/ppermute | solution.py:216
  56.7 1.5 %collective-permute-start.24 = (bf16[640,128]{1,0:T(8,128)(2,1)S(1)}, bf16[640,128]{1,0:T(8,128)(2,1)S(1)}, u32[]{:S(2)}, u32[]{:S(2)}) collective-permute-start(bf16[640,128]{1,0:T(8,128)(2,1)S(1)} %get-tuple-element.77.old_upper), channel_id=1, source_target_pairs={{0,16},{16,0},{1,17},{17,1},{2,18},{18,2},{3,19},{19,3},{4,20},{20... | collective-permute-start | bytes 491528 | tf_op jit(solution)/shard_map/ppermute | solution.py:216
  58.2 1.5 %collective-permute-start.23 = (bf16[640,128]{1,0:T(8,128)(2,1)S(1)}, bf16[640,128]{1,0:T(8,128)(2,1)S(1)}, u32[]{:S(2)}, u32[]{:S(2)}) collective-permute-start(bf16[640,128]{1,0:T(8,128)(2,1)S(1)} %get-tuple-element.80.old_right), channel_id=1, source_target_pairs={{0,2},{1,3},{2,4},{3,5},{4,6},{5,7},{6,8},{7,9},{8,10},{9,11},{10,... | collective-permute-start | bytes 491528 | tf_op jit(solution)/shard_map/ppermute | solution.py:213
  60.4 1.5 %collective-permute-start.22 = (bf16[640,128]{1,0:T(8,128)(2,1)S(1)}, bf16[640,128]{1,0:T(8,128)(2,1)S(1)}, u32[]{:S(2)}, u32[]{:S(2)}) collective-permute-start(bf16[640,128]{1,0:T(8,128)(2,1)S(1)} %get-tuple-element.82), channel_id=1, source_target_pairs={{0,2},{1,3},{2,4},{3,5},{4,6},{5,7},{6,8},{7,9},{8,10},{9,11},{10,... | collective-permute-start | bytes 491528 | tf_op jit(solution)/shard_map/ppermute | solution.py:213
  63.2 4.8 %collective-permute-done.23.right_in = bf16[640,128]{1,0:T(8,128)(2,1)S(1)} collective-permute-done((bf16[640,128]{1,0:T(8,128)(2,1)S(1)}, bf16[640,128]{1,0:T(8,128)(2,1)S(1)}, u32[]{:S(2)}, u32[]{:S(2)}) %collective-permute-start.23) | collective-permute-done | bytes 163872 | tf_op jit(solution)/shard_map/ppermute | solution.py:213
  68.7 2.0 %collective-permute-done.22.second.first = bf16[640,128]{1,0:T(8,128)(2,1)S(1)} collective-permute-done((bf16[640,128]{1,0:T(8,128)(2,1)S(1)}, bf16[640,128]{1,0:T(8,128)(2,1)S(1)}, u32[]{:S(2)}, u32[]{:S(2)}) %collective-permute-start.22) | collective-permute-done | bytes 163872 | tf_op jit(solution)/shard_map/ppermute | solution.py:213
  72.9 1.5 %last.1 = bf16[1280,256]{1,0:T(8,128)(2,1)} custom-call(bf16[1280,1280]{1,0:T(8,128)(2,1)S(1)} %get-tuple-element.45.own.mapping, f32[1280,256]{1,0:T(8,128)S(1)} %shard_map.48.total, bf16[640,256]{1,0:T(8,128)(2,1)S(1)} %collective-permute-done.27.upper_in), custom_call_target="tpu_custom_call" | custom-call | flops 400000000 | bytes 2000000 | tf_op jit(solution)/shard_map/last/pallas_call | solution.py:184
  (58 shorter events, 25.7 us)
Async XLA Ops:
  0.0 12.3 %collective-permute-start = (bf16[1280,1280]{1,0:T(8,128)(2,1)}, bf16[1280,1280]{1,0:T(8,128)(2,1)S(1)}, u32[]{:S(2)}, u32[]{:S(2)}) collective-permute-start(bf16[1280,1280]{1,0:T(8,128)(2,1)} %bitcast.3), channel_id=1, source_target_pairs={{0,1},{1,0},{2,3},{3,2},{4,5},{5,4},{6,7},{7,6},{8,9},{9,8},{10,11... | collective-permute-start | bytes 9830408 | tf_op jit(solution)/shard_map/ppermute | solution.py:210
  7.3 10.5 %collective-permute-start.2 = (bf16[640,128]{1,0:T(8,128)(2,1)S(1)}, bf16[640,128]{1,0:T(8,128)(2,1)S(1)}, u32[]{:S(2)}, u32[]{:S(2)}) collective-permute-start(bf16[640,128]{1,0:T(8,128)(2,1)S(1)} %get-tuple-element.49.old_right), channel_id=1, source_target_pairs={{0,2},{1,3},{2,4},{3,5},{4,6},{5,7},{6,8},{7,9},{8,10},{9,11},{10,... | collective-permute-start | bytes 491528 | tf_op jit(solution)/shard_map/ppermute | solution.py:213
  10.3 8.2 %collective-permute-start.3 = (bf16[640,128]{1,0:T(8,128)(2,1)S(1)}, bf16[640,128]{1,0:T(8,128)(2,1)S(1)}, u32[]{:S(2)}, u32[]{:S(2)}) collective-permute-start(bf16[640,128]{1,0:T(8,128)(2,1)S(1)} %get-tuple-element.54.old_upper), channel_id=1, source_target_pairs={{0,16},{16,0},{1,17},{17,1},{2,18},{18,2},{3,19},{19,3},{4,20},{20... | collective-permute-start | bytes 491528 | tf_op jit(solution)/shard_map/ppermute | solution.py:216
  11.8 9.2 %collective-permute-start.7 = (bf16[640,128]{1,0:T(8,128)(2,1)S(1)}, bf16[640,128]{1,0:T(8,128)(2,1)S(1)}, u32[]{:S(2)}, u32[]{:S(2)}) collective-permute-start(bf16[640,128]{1,0:T(8,128)(2,1)S(1)} %get-tuple-element.52.old_upper), channel_id=1, source_target_pairs={{0,16},{16,0},{1,17},{17,1},{2,18},{18,2},{3,19},{19,3},{4,20},{20... | collective-permute-start | bytes 491528 | tf_op jit(solution)/shard_map/ppermute | solution.py:216
  13.4 8.9 %collective-permute-start.6 = (bf16[640,128]{1,0:T(8,128)(2,1)S(1)}, bf16[640,128]{1,0:T(8,128)(2,1)S(1)}, u32[]{:S(2)}, u32[]{:S(2)}) collective-permute-start(bf16[640,128]{1,0:T(8,128)(2,1)S(1)} %get-tuple-element.56.old_right), channel_id=1, source_target_pairs={{0,2},{1,3},{2,4},{3,5},{4,6},{5,7},{6,8},{7,9},{8,10},{9,11},{10,... | collective-permute-start | bytes 491528 | tf_op jit(solution)/shard_map/ppermute | solution.py:213
  15.0 9.4 %collective-permute-start.9 = (bf16[640,128]{1,0:T(8,128)(2,1)S(1)}, bf16[640,128]{1,0:T(8,128)(2,1)S(1)}, u32[]{:S(2)}, u32[]{:S(2)}) collective-permute-start(bf16[640,128]{1,0:T(8,128)(2,1)S(1)} %get-tuple-element.57.old_upper), channel_id=1, source_target_pairs={{0,16},{16,0},{1,17},{17,1},{2,18},{18,2},{3,19},{19,3},{4,20},{20... | collective-permute-start | bytes 491528 | tf_op jit(solution)/shard_map/ppermute | solution.py:216
  19.1 9.0 %collective-permute-start.4 = (bf16[640,128]{1,0:T(8,128)(2,1)S(1)}, bf16[640,128]{1,0:T(8,128)(2,1)S(1)}, u32[]{:S(2)}, u32[]{:S(2)}) collective-permute-start(bf16[640,128]{1,0:T(8,128)(2,1)S(1)} %get-tuple-element.58.old_right), channel_id=1, source_target_pairs={{0,2},{1,3},{2,4},{3,5},{4,6},{5,7},{6,8},{7,9},{8,10},{9,11},{10,... | collective-permute-start | bytes 491528 | tf_op jit(solution)/shard_map/ppermute | solution.py:213
  19.5 9.1 %collective-permute-start.5 = (bf16[640,128]{1,0:T(8,128)(2,1)S(1)}, bf16[640,128]{1,0:T(8,128)(2,1)S(1)}, u32[]{:S(2)}, u32[]{:S(2)}) collective-permute-start(bf16[640,128]{1,0:T(8,128)(2,1)S(1)} %get-tuple-element.59.old_upper), channel_id=1, source_target_pairs={{0,16},{16,0},{1,17},{17,1},{2,18},{18,2},{3,19},{19,3},{4,20},{20... | collective-permute-start | bytes 491528 | tf_op jit(solution)/shard_map/ppermute | solution.py:216
  21.0 10.4 %collective-permute-start.8 = (bf16[640,128]{1,0:T(8,128)(2,1)S(1)}, bf16[640,128]{1,0:T(8,128)(2,1)S(1)}, u32[]{:S(2)}, u32[]{:S(2)}) collective-permute-start(bf16[640,128]{1,0:T(8,128)(2,1)S(1)} %get-tuple-element.63.old_upper), channel_id=1, source_target_pairs={{0,16},{16,0},{1,17},{17,1},{2,18},{18,2},{3,19},{19,3},{4,20},{20... | collective-permute-start | bytes 491528 | tf_op jit(solution)/shard_map/ppermute | solution.py:216
  25.0 10.1 %collective-permute-start.12 = (bf16[640,128]{1,0:T(8,128)(2,1)S(1)}, bf16[640,128]{1,0:T(8,128)(2,1)S(1)}, u32[]{:S(2)}, u32[]{:S(2)}) collective-permute-start(bf16[640,128]{1,0:T(8,128)(2,1)S(1)} %get-tuple-element.64.old_right), channel_id=1, source_target_pairs={{0,2},{1,3},{2,4},{3,5},{4,6},{5,7},{6,8},{7,9},{8,10},{9,11},{10,... | collective-permute-start | bytes 491528 | tf_op jit(solution)/shard_map/ppermute | solution.py:213
  26.5 9.1 %collective-permute-start.13 = (bf16[640,128]{1,0:T(8,128)(2,1)S(1)}, bf16[640,128]{1,0:T(8,128)(2,1)S(1)}, u32[]{:S(2)}, u32[]{:S(2)}) collective-permute-start(bf16[640,128]{1,0:T(8,128)(2,1)S(1)} %get-tuple-element.61.old_upper), channel_id=1, source_target_pairs={{0,16},{16,0},{1,17},{17,1},{2,18},{18,2},{3,19},{19,3},{4,20},{20... | collective-permute-start | bytes 491528 | tf_op jit(solution)/shard_map/ppermute | solution.py:216
  28.0 10.4 %collective-permute-start.15 = (bf16[640,128]{1,0:T(8,128)(2,1)S(1)}, bf16[640,128]{1,0:T(8,128)(2,1)S(1)}, u32[]{:S(2)}, u32[]{:S(2)}) collective-permute-start(bf16[640,128]{1,0:T(8,128)(2,1)S(1)} %get-tuple-element.65.old_upper), channel_id=1, source_target_pairs={{0,16},{16,0},{1,17},{17,1},{2,18},{18,2},{3,19},{19,3},{4,20},{20... | collective-permute-start | bytes 491528 | tf_op jit(solution)/shard_map/ppermute | solution.py:216
  32.0 10.1 %collective-permute-start.10 = (bf16[640,128]{1,0:T(8,128)(2,1)S(1)}, bf16[640,128]{1,0:T(8,128)(2,1)S(1)}, u32[]{:S(2)}, u32[]{:S(2)}) collective-permute-start(bf16[640,128]{1,0:T(8,128)(2,1)S(1)} %get-tuple-element.66.old_right), channel_id=1, source_target_pairs={{0,2},{1,3},{2,4},{3,5},{4,6},{5,7},{6,8},{7,9},{8,10},{9,11},{10,... | collective-permute-start | bytes 491528 | tf_op jit(solution)/shard_map/ppermute | solution.py:213
  33.6 9.1 %collective-permute-start.11 = (bf16[640,128]{1,0:T(8,128)(2,1)S(1)}, bf16[640,128]{1,0:T(8,128)(2,1)S(1)}, u32[]{:S(2)}, u32[]{:S(2)}) collective-permute-start(bf16[640,128]{1,0:T(8,128)(2,1)S(1)} %get-tuple-element.67.old_upper), channel_id=1, source_target_pairs={{0,16},{16,0},{1,17},{17,1},{2,18},{18,2},{3,19},{19,3},{4,20},{20... | collective-permute-start | bytes 491528 | tf_op jit(solution)/shard_map/ppermute | solution.py:216
  35.0 10.4 %collective-permute-start.14 = (bf16[640,128]{1,0:T(8,128)(2,1)S(1)}, bf16[640,128]{1,0:T(8,128)(2,1)S(1)}, u32[]{:S(2)}, u32[]{:S(2)}) collective-permute-start(bf16[640,128]{1,0:T(8,128)(2,1)S(1)} %get-tuple-element.71.old_upper), channel_id=1, source_target_pairs={{0,16},{16,0},{1,17},{17,1},{2,18},{18,2},{3,19},{19,3},{4,20},{20... | collective-permute-start | bytes 491528 | tf_op jit(solution)/shard_map/ppermute | solution.py:216
  39.0 10.1 %collective-permute-start.18 = (bf16[640,128]{1,0:T(8,128)(2,1)S(1)}, bf16[640,128]{1,0:T(8,128)(2,1)S(1)}, u32[]{:S(2)}, u32[]{:S(2)}) collective-permute-start(bf16[640,128]{1,0:T(8,128)(2,1)S(1)} %get-tuple-element.72.old_right), channel_id=1, source_target_pairs={{0,2},{1,3},{2,4},{3,5},{4,6},{5,7},{6,8},{7,9},{8,10},{9,11},{10,... | collective-permute-start | bytes 491528 | tf_op jit(solution)/shard_map/ppermute | solution.py:213
  40.6 9.1 %collective-permute-start.19 = (bf16[640,128]{1,0:T(8,128)(2,1)S(1)}, bf16[640,128]{1,0:T(8,128)(2,1)S(1)}, u32[]{:S(2)}, u32[]{:S(2)}) collective-permute-start(bf16[640,128]{1,0:T(8,128)(2,1)S(1)} %get-tuple-element.69.old_upper), channel_id=1, source_target_pairs={{0,16},{16,0},{1,17},{17,1},{2,18},{18,2},{3,19},{19,3},{4,20},{20... | collective-permute-start | bytes 491528 | tf_op jit(solution)/shard_map/ppermute | solution.py:216
  42.1 10.4 %collective-permute-start.21 = (bf16[640,128]{1,0:T(8,128)(2,1)S(1)}, bf16[640,128]{1,0:T(8,128)(2,1)S(1)}, u32[]{:S(2)}, u32[]{:S(2)}) collective-permute-start(bf16[640,128]{1,0:T(8,128)(2,1)S(1)} %get-tuple-element.73.old_upper), channel_id=1, source_target_pairs={{0,16},{16,0},{1,17},{17,1},{2,18},{18,2},{3,19},{19,3},{4,20},{20... | collective-permute-start | bytes 491528 | tf_op jit(solution)/shard_map/ppermute | solution.py:216
  47.6 8.4 %collective-permute-start.17 = (bf16[640,128]{1,0:T(8,128)(2,1)S(1)}, bf16[640,128]{1,0:T(8,128)(2,1)S(1)}, u32[]{:S(2)}, u32[]{:S(2)}) collective-permute-start(bf16[640,128]{1,0:T(8,128)(2,1)S(1)} %get-tuple-element.75.old_upper), channel_id=1, source_target_pairs={{0,16},{16,0},{1,17},{17,1},{2,18},{18,2},{3,19},{19,3},{4,20},{20... | collective-permute-start | bytes 491528 | tf_op jit(solution)/shard_map/ppermute | solution.py:216
  49.1 10.7 %collective-permute-start.20 = (bf16[640,128]{1,0:T(8,128)(2,1)S(1)}, bf16[640,128]{1,0:T(8,128)(2,1)S(1)}, u32[]{:S(2)}, u32[]{:S(2)}) collective-permute-start(bf16[640,128]{1,0:T(8,128)(2,1)S(1)} %get-tuple-element.79.old_upper), channel_id=1, source_target_pairs={{0,16},{16,0},{1,17},{17,1},{2,18},{18,2},{3,19},{19,3},{4,20},{20... | collective-permute-start | bytes 491528 | tf_op jit(solution)/shard_map/ppermute | solution.py:216
  56.7 11.3 %collective-permute-start.24 = (bf16[640,128]{1,0:T(8,128)(2,1)S(1)}, bf16[640,128]{1,0:T(8,128)(2,1)S(1)}, u32[]{:S(2)}, u32[]{:S(2)}) collective-permute-start(bf16[640,128]{1,0:T(8,128)(2,1)S(1)} %get-tuple-element.77.old_upper), channel_id=1, source_target_pairs={{0,16},{16,0},{1,17},{17,1},{2,18},{18,2},{3,19},{19,3},{4,20},{20... | collective-permute-start | bytes 491528 | tf_op jit(solution)/shard_map/ppermute | solution.py:216
  58.2 9.8 %collective-permute-start.23 = (bf16[640,128]{1,0:T(8,128)(2,1)S(1)}, bf16[640,128]{1,0:T(8,128)(2,1)S(1)}, u32[]{:S(2)}, u32[]{:S(2)}) collective-permute-start(bf16[640,128]{1,0:T(8,128)(2,1)S(1)} %get-tuple-element.80.old_right), channel_id=1, source_target_pairs={{0,2},{1,3},{2,4},{3,5},{4,6},{5,7},{6,8},{7,9},{8,10},{9,11},{10,... | collective-permute-start | bytes 491528 | tf_op jit(solution)/shard_map/ppermute | solution.py:213
  60.4 10.3 %collective-permute-start.22 = (bf16[640,128]{1,0:T(8,128)(2,1)S(1)}, bf16[640,128]{1,0:T(8,128)(2,1)S(1)}, u32[]{:S(2)}, u32[]{:S(2)}) collective-permute-start(bf16[640,128]{1,0:T(8,128)(2,1)S(1)} %get-tuple-element.82), channel_id=1, source_target_pairs={{0,2},{1,3},{2,4},{3,5},{4,6},{5,7},{6,8},{7,9},{8,10},{9,11},{10,... | collective-permute-start | bytes 491528 | tf_op jit(solution)/shard_map/ppermute | solution.py:213
  62.0 10.9 %collective-permute-start.27 = (bf16[640,256]{1,0:T(8,128)(2,1)S(1)}, bf16[640,256]{1,0:T(8,128)(2,1)S(1)}, u32[]{:S(2)}, u32[]{:S(2)}) collective-permute-start(bf16[640,256]{1,0:T(8,128)(2,1)S(1)} %shard_map.50), channel_id=1, source_target_pairs={{0,16},{16,0},{1,17},{17,1},{2,18},{18,2},{3,19},{19,3},{4,20},{20... | collective-permute-start | bytes 983048 | tf_op jit(solution)/shard_map/ppermute | solution.py:216
  (4 other events, 21.5 us)
where the time goes:
time: 74.8 us; the launch traced here: 74.6 us
  starting transfers between devices  31.5 us (42%)
  waiting for transfers between devices  27.5 us (37%)
  Pallas kernels  15.2 us (20%)
    ppermute x15, starting transfers between devices, upward(): return lax.ppermute(array, 'row', up)  16.6 us
    ppermute x9, starting transfers between devices, rightward(): return lax.ppermute(array, 'col', cross)  14.3 us
    ppermute x15, waiting for transfers between devices, upward(): return lax.ppermute(array, 'row', up)  11.9 us
    pallas_call x23, Pallas kernels, call(): pl.pallas_call(body, out_shape=[pltpu.VMEM(*(out if isinstance(out[0], tu...  11.5 us
    ppermute x9, waiting for transfers between devices, rightward(): return lax.ppermute(array, 'col', cross)  9.73 us
    ppermute x4, waiting for transfers between devices, exchange(): return lax.ppermute(array, 'col', swap)  5.83 us
    pallas_call x1, Pallas kernels, load(): pl.pallas_call(load_body, out_shape=[pltpu.VMEM(array.shape, array.dtype)...  2.15 us
    pallas_call x1, Pallas kernels, last(): pl.pallas_call(last_body, out_shape=jax.ShapeDtypeStruct(shape, jnp.bfloa...  1.54 us
  transfers between devices with their start and end apart: 28, of which 12 were waited for; matrix products, arithmetic and copies ran while one was open for 0% of the time, Pallas kernels for 18%

commit v1 on v0

--- a/solution.py
+++ b/solution.py
@@ -36,10 +36,29 @@
     return jnp.dot(left, right, preferred_element_type=jnp.float32)
 
 
-def load_body(mapping, source, map_own, source_own, sems):
+def fetch(body, outs, operand):
+    return pl.pallas_call(
+        body,
+        out_shape=[pltpu.VMEM(shape, operand.dtype) for shape in outs],
+        in_specs=[pl.BlockSpec(memory_space=pltpu.HBM)],
+        out_specs=[VMEM] * len(outs),
+        scratch_shapes=[pltpu.SemaphoreType.DMA((len(outs),))],
+        compiler_params=pltpu.CompilerParams(vmem_limit_bytes=LIMIT),
+        cost_estimate=COST,
+    )(pltpu.with_memory_space_constraint(operand, pltpu.HBM))
+
+
+def load_map_body(mapping, map_own, sems):
+    copy = pltpu.make_async_copy(mapping, map_own, sems.at[0])
+    copy.start()
+    copy.wait()
+
+
+def load_source_body(source, upper, source_own, sems):
+    half = upper.shape[0]
     copies = [
-        pltpu.make_async_copy(source, source_own, sems.at[0]),
-        pltpu.make_async_copy(mapping, map_own, sems.at[1]),
+        pltpu.make_async_copy(source.at[half:, :], upper, sems.at[0]),
+        pltpu.make_async_copy(source, source_own, sems.at[1]),
     ]
     for copy in copies:
         copy.start()
@@ -47,17 +66,23 @@
         copy.wait()
 
 
-def load(mapping, source):
-    return pl.pallas_call(
-        load_body,
-        out_shape=[pltpu.VMEM(array.shape, array.dtype) for array in (mapping, source)],
-        in_specs=[pl.BlockSpec(memory_space=pltpu.HBM)] * 2,
-        out_specs=[VMEM] * 2,
-        scratch_shapes=[pltpu.SemaphoreType.DMA((2,))],
-        compiler_params=pltpu.CompilerParams(vmem_limit_bytes=LIMIT),
-        cost_estimate=COST,
-        name="load",
-    )(*[pltpu.with_memory_space_constraint(array, pltpu.HBM) for array in (mapping, source)])
+def halve_body(whole, kept, sent):
+    width = kept.shape[1]
+    core = lax.rem(lax.axis_index("col"), 2)
+    for k in range(2):
+        @pl.when(core == k)
+        def _():
+            kept[...] = whole[:, k * width:(k + 1) * width]
+            sent[...] = whole[:, (1 - k) * width:(2 - k) * width]
+
+
+def order_body(own, got, first, second):
+    core = lax.rem(lax.axis_index("col"), 2)
+    for k in range(2):
+        @pl.when(core == k)
+        def _():
+            first[...] = own[...] if k == 0 else got[...]
+            second[...] = got[...] if k == 0 else own[...]
 
 
 def pick_body(own, got, source_a, source_b, right_a, upper_a, right_b, upper_b):
@@ -157,21 +182,21 @@
         whole[:, width:] = second[...]
 
 
-def begin_body(mapping, right_in, source, total):
+def begin_body(mapping, upper_in, source, total):
+    half = upper_in.shape[0]
+    below = jnp.where(lax.axis_index("row") == 0, jnp.zeros_like(upper_in), upper_in[...])
+    total[...] = dot(mapping[:, half:], below) + source[...].astype(jnp.float32)
+
+
+def last_body(mapping, total, right_in, out, ready, sems):
     half = right_in.shape[0]
-    left = jnp.where(lax.axis_index("col") == 0, jnp.zeros_like(right_in), right_in[...])
-    total[...] = dot(mapping[:, :half], left) + source[...].astype(jnp.float32)
-
-
-def last_body(mapping, total, upper_in, out, ready, sems):
-    half = upper_in.shape[0]
     parts = sems.shape[0]
     tall = total.shape[0] // parts
     copies = []
-    below = jnp.where(lax.axis_index("row") == 0, jnp.zeros_like(upper_in), upper_in[...])
+    left = jnp.where(lax.axis_index("col") == 0, jnp.zeros_like(right_in), right_in[...])
     for n in range(parts):
         rows = slice(n * tall, (n + 1) * tall)
-        ready[rows, :] = (total[rows, :] + dot(mapping[rows, half:], below)).astype(ready.dtype)
+        ready[rows, :] = (total[rows, :] + dot(mapping[rows, :half], left)).astype(ready.dtype)
         copy = pltpu.make_async_copy(ready.at[rows, :], out.at[rows, :], sems.at[n])
         copy.start()
         copies.append(copy)
@@ -179,14 +204,14 @@
         copy.wait()
 
 
-def last(mapping, total, upper_in, shape):
-    operands = [in_vmem(operand) for operand in (mapping, total, upper_in)]
+def last(mapping, total, right_in, shape):
+    operands = [in_vmem(operand) for operand in (mapping, total, right_in)]
     return pl.pallas_call(
         last_body,
         out_shape=jax.ShapeDtypeStruct(shape, jnp.bfloat16),
         in_specs=[VMEM] * 3,
         out_specs=pl.BlockSpec(memory_space=pltpu.HBM),
-        scratch_shapes=[pltpu.VMEM(shape, jnp.bfloat16), pltpu.SemaphoreType.DMA((2,))],
+        scratch_shapes=[pltpu.VMEM(shape, jnp.bfloat16), pltpu.SemaphoreType.DMA((4,))],
         compiler_params=pltpu.CompilerParams(vmem_limit_bytes=LIMIT),
         cost_estimate=COST,
         name="last",
@@ -209,21 +234,21 @@
     def exchange(array):
         return lax.ppermute(array, "col", swap)
 
-    def rightward(array):
-        return lax.ppermute(array, "col", cross)
+    def rightward(array, wrap=True):
+        return lax.ppermute(array, "col", cross if wrap else cross[:-2])
 
     def upward(array):
         return lax.ppermute(array, "row", up)
 
     source_got = exchange(source)
     map_got = exchange(mapping)
-    map_own, source_own = load(mapping, source)
     trace, state = (half, part), (order, part)
+    upper_own, source_own = fetch(load_source_body, [(half, width), (order, width)], source)
+    below_own = upward(upper_own)
+    map_own, = fetch(load_map_body, [(order, order)], mapping)
     source_a, source_b, right_a, upper_a, right_b, upper_b = call(
         pick_body, [state] * 2 + [trace] * 4, source_own, source_got)
-    below_b = [upward(upper_b)]
     left = rightward(right_b)
-    below_a = [upward(upper_a)]
     map_a, map_b = call(sort_body, [(order, order)] * 2, map_own, map_got)
 
     def advance(column, slot, *operands):
@@ -231,12 +256,16 @@
         return call(body, [trace] * 2, *operands)
 
     zero = jnp.zeros(trace, jnp.bfloat16)
+    below_a, below_b = [None], [None]
     for slot in range(slots):
         message = slot - 1 - LAG
+        if message == -1:
+            kept, sent = call(halve_body, [trace] * 2, below_own)
+            below_a[0], below_b[0] = call(order_body, [trace] * 2, kept, exchange(sent))
         in_b = below_b[message + 1] if message >= -1 else zero
         in_a = below_a[message + 1] if message >= -1 else zero
         new_right_b, upper_b = advance("b", slot, map_b, right_a, in_b, source_b, right_b, upper_b)
-        new_left = rightward(new_right_b)
+        new_left = rightward(new_right_b, wrap=slot < slots - 1)
         if slot < last_message:
             below_b.append(upward(upper_b))
         right_a, upper_a = advance("a", slot, map_a, left, in_a, source_a, right_a, upper_a)
@@ -249,9 +278,10 @@
         right_b, left = new_right_b, new_left
 
     given, = call(give_body, [trace], right_a, left)
-    right_in, = call(join_body, [(half, width)], left, right_a, exchange(given))
-    total, = call(begin_body, [((order, width), jnp.float32)], map_own, right_in, source_own)
-    out = last(map_own, total, below_last, (order, width))
+    got = exchange(given)
+    total, = call(begin_body, [((order, width), jnp.float32)], map_own, below_last, source_own)
+    right_in, = call(join_body, [(half, width)], left, right_a, got)
+    out = last(map_own, total, right_in, (order, width))
     return out[None, None]
 
 

time: 74.8 us -> 77.6 us (1.037)
  waiting for transfers between devices: 27.5 us -> 32.6 us
  starting transfers between devices: 31.5 us -> 28.3 us
  Pallas kernels: 15.2 us -> 16.1 us
    ppermute x15 -> x14, waiting for transfers between devices: 11.9 us -> 21.2 us  [upward(): return lax.ppermute(array, 'row', up)]
    ppermute x4 -> x5, waiting for transfers between devices: 5.83 us -> 1.39 us  [exchange(): return lax.ppermute(array, 'col', swap)]
    ppermute x9, starting transfers between devices: 14.3 us -> 10.7 us  [rightward(): return lax.ppermute(array, 'col', cross if wrap else cross[:-2])]
    pallas_call x1 -> x2, Pallas kernels: 2.15 us -> 3.14 us  [fetch(): pl.pallas_call(body, out_shape=[pltpu.VMEM(shape, operand.dtype) for shap...]
    ppermute x15 -> x14, starting transfers between devices: 16.6 us -> 16.8 us  [upward(): return lax.ppermute(array, 'row', up)]
    pallas_call x23 -> x25, Pallas kernels: 11.5 us -> 11.5 us  [call(): pl.pallas_call(body, out_shape=[pltpu.VMEM(*(out if isinstance(out[0], tu...]
  transfers between devices with their start and end apart: 28 -> 28, of which waited for: 12 -> 13; matrix products, arithmetic and copies ran while one was open for 0% -> 0% of each run, Pallas kernels for 18% -> 18%
where the time goes in v1:
time: 77.6 us; the launch traced here: 77.4 us
  waiting for transfers between devices  32.6 us (42%)
  starting transfers between devices  28.3 us (36%)
  Pallas kernels  16.1 us (21%)
    ppermute x14, waiting for transfers between devices, upward(): return lax.ppermute(array, 'row', up)  21.2 us
    ppermute x14, starting transfers between devices, upward(): return lax.ppermute(array, 'row', up)  16.8 us
    pallas_call x25, Pallas kernels, call(): pl.pallas_call(body, out_shape=[pltpu.VMEM(*(out if isinstance(out[0], tu...  11.5 us
    ppermute x9, starting transfers between devices, rightward(): return lax.ppermute(array, 'col', cross if wrap else cross[:-2])  10.7 us
    ppermute x9, waiting for transfers between devices, rightward(): return lax.ppermute(array, 'col', cross if wrap else cross[:-2])  9.99 us
    pallas_call x2, Pallas kernels, fetch(): pl.pallas_call(body, out_shape=[pltpu.VMEM(shape, operand.dtype) for shap...  3.14 us
  transfers between devices with their start and end apart: 28, of which 13 were waited for; matrix products, arithmetic and copies ran while one was open for 0% of the time, Pallas kernels for 18%

profile of v1, /device:TPU:0, one launch (start us, length us, event | category | flops | bytes accessed | tf_op | source)
XLA Modules:
  0.0 77.4 jit_solution(1060487416329213193)
XLA Ops:
  0.5 1.2 %shard_map.30 = (bf16[640,256]{1,0:T(8,128)(2,1)S(1)}, bf16[1280,256]{1,0:T(8,128)(2,1)S(1)}) custom-call(bf16[1280,256]{1,0:T(8,128)(2,1)} %bitcast.6), custom_call_target="tpu_custom_call" | custom-call | flops 400000000 | bytes 2000000 | tf_op jit(solution)/shard_map/pallas_call | solution.py:40
  1.7 3.0 %collective-permute-start.3 = (bf16[640,256]{1,0:T(8,128)(2,1)S(1)}, bf16[640,256]{1,0:T(8,128)(2,1)S(1)}, u32[]{:S(2)}, u32[]{:S(2)}) collective-permute-start(bf16[640,256]{1,0:T(8,128)(2,1)S(1)} %get-tuple-element.57), channel_id=1, source_target_pairs={{0,16},{16,0},{1,17},{17,1},{2,18},{18,2},{3,19},{19,3},{4,20},{20... | collective-permute-start | bytes 983048 | tf_op jit(solution)/shard_map/ppermute | solution.py:241
  4.8 7.9 %collective-permute-done.3.whole = bf16[640,256]{1,0:T(8,128)(2,1)S(1)} collective-permute-done((bf16[640,256]{1,0:T(8,128)(2,1)S(1)}, bf16[640,256]{1,0:T(8,128)(2,1)S(1)}, u32[]{:S(2)}, u32[]{:S(2)}) %collective-permute-start.3) | collective-permute-done | bytes 327712 | tf_op jit(solution)/shard_map/ppermute | solution.py:241
  13.0 1.8 %collective-permute-start.2 = (bf16[640,128]{1,0:T(8,128)(2,1)S(1)}, bf16[640,128]{1,0:T(8,128)(2,1)S(1)}, u32[]{:S(2)}, u32[]{:S(2)}) collective-permute-start(bf16[640,128]{1,0:T(8,128)(2,1)S(1)} %get-tuple-element.52.old_right), channel_id=1, source_target_pairs={{0,2},{1,3},{2,4},{3,5},{4,6},{5,7},{6,8},{7,9},{8,10},{9,11},{10,... | collective-permute-start | bytes 491528 | tf_op jit(solution)/shard_map/ppermute | solution.py:238
  14.9 1.9 %shard_map.28.own.mapping = bf16[1280,1280]{1,0:T(8,128)(2,1)S(1)} custom-call(bf16[1280,1280]{1,0:T(8,128)(2,1)} %bitcast.4), custom_call_target="tpu_custom_call" | custom-call | flops 400000000 | bytes 2000000 | tf_op jit(solution)/shard_map/pallas_call | solution.py:40
  18.0 1.6 %collective-permute-start.7 = (bf16[640,128]{1,0:T(8,128)(2,1)S(1)}, bf16[640,128]{1,0:T(8,128)(2,1)S(1)}, u32[]{:S(2)}, u32[]{:S(2)}) collective-permute-start(bf16[640,128]{1,0:T(8,128)(2,1)S(1)} %get-tuple-element.63.old_right), channel_id=1, source_target_pairs={{0,2},{1,3},{2,4},{3,5},{4,6},{5,7},{6,8},{7,9},{8,10},{9,11},{10,... | collective-permute-start | bytes 491528 | tf_op jit(solution)/shard_map/ppermute | solution.py:238
  20.5 2.3 %collective-permute-done.2.right_in = bf16[640,128]{1,0:T(8,128)(2,1)S(1)} collective-permute-done((bf16[640,128]{1,0:T(8,128)(2,1)S(1)}, bf16[640,128]{1,0:T(8,128)(2,1)S(1)}, u32[]{:S(2)}, u32[]{:S(2)}) %collective-permute-start.2) | collective-permute-done | bytes 163872 | tf_op jit(solution)/shard_map/ppermute | solution.py:238
  25.0 1.1 %collective-permute-start.8 = (bf16[640,128]{1,0:T(8,128)(2,1)S(1)}, bf16[640,128]{1,0:T(8,128)(2,1)S(1)}, u32[]{:S(2)}, u32[]{:S(2)}) collective-permute-start(bf16[640,128]{1,0:T(8,128)(2,1)S(1)} %get-tuple-element.71.old_upper), channel_id=1, source_target_pairs={{0,16},{16,0},{1,17},{17,1},{2,18},{18,2},{3,19},{19,3},{4,20},{20... | collective-permute-start | bytes 491528 | tf_op jit(solution)/shard_map/ppermute | solution.py:241
  29.3 3.4 %collective-permute-done.5.right_in = bf16[640,128]{1,0:T(8,128)(2,1)S(1)} collective-permute-done((bf16[640,128]{1,0:T(8,128)(2,1)S(1)}, bf16[640,128]{1,0:T(8,128)(2,1)S(1)}, u32[]{:S(2)}, u32[]{:S(2)}) %collective-permute-start.5) | collective-permute-done | bytes 163872 | tf_op jit(solution)/shard_map/ppermute | solution.py:238
  37.3 1.1 %collective-permute-start.14 = (bf16[640,128]{1,0:T(8,128)(2,1)S(1)}, bf16[640,128]{1,0:T(8,128)(2,1)S(1)}, u32[]{:S(2)}, u32[]{:S(2)}) collective-permute-start(bf16[640,128]{1,0:T(8,128)(2,1)S(1)} %get-tuple-element.79.old_upper), channel_id=1, source_target_pairs={{0,16},{16,0},{1,17},{17,1},{2,18},{18,2},{3,19},{19,3},{4,20},{20... | collective-permute-start | bytes 491528 | tf_op jit(solution)/shard_map/ppermute | solution.py:241
  39.0 2.7 %collective-permute-done.15.upper_in = bf16[640,128]{1,0:T(8,128)(2,1)S(1)} collective-permute-done((bf16[640,128]{1,0:T(8,128)(2,1)S(1)}, bf16[640,128]{1,0:T(8,128)(2,1)S(1)}, u32[]{:S(2)}, u32[]{:S(2)}) %collective-permute-start.15) | collective-permute-done | bytes 163872 | tf_op jit(solution)/shard_map/ppermute | solution.py:241
  42.3 1.1 %collective-permute-start.18 = (bf16[640,128]{1,0:T(8,128)(2,1)S(1)}, bf16[640,128]{1,0:T(8,128)(2,1)S(1)}, u32[]{:S(2)}, u32[]{:S(2)}) collective-permute-start(bf16[640,128]{1,0:T(8,128)(2,1)S(1)} %get-tuple-element.80.old_right), channel_id=1, source_target_pairs={{0,2},{1,3},{2,4},{3,5},{4,6},{5,7},{6,8},{7,9},{8,10},{9,11},{10,... | collective-permute-start | bytes 491528 | tf_op jit(solution)/shard_map/ppermute | solution.py:238
  44.3 1.1 %collective-permute-start.20 = (bf16[640,128]{1,0:T(8,128)(2,1)S(1)}, bf16[640,128]{1,0:T(8,128)(2,1)S(1)}, u32[]{:S(2)}, u32[]{:S(2)}) collective-permute-start(bf16[640,128]{1,0:T(8,128)(2,1)S(1)} %get-tuple-element.81.old_upper), channel_id=1, source_target_pairs={{0,16},{16,0},{1,17},{17,1},{2,18},{18,2},{3,19},{19,3},{4,20},{20... | collective-permute-start | bytes 491528 | tf_op jit(solution)/shard_map/ppermute | solution.py:241
  46.0 2.7 %collective-permute-done.14.upper_in = bf16[640,128]{1,0:T(8,128)(2,1)S(1)} collective-permute-done((bf16[640,128]{1,0:T(8,128)(2,1)S(1)}, bf16[640,128]{1,0:T(8,128)(2,1)S(1)}, u32[]{:S(2)}, u32[]{:S(2)}) %collective-permute-start.14) | collective-permute-done | bytes 163872 | tf_op jit(solution)/shard_map/ppermute | solution.py:241
  49.3 1.1 %collective-permute-start.16 = (bf16[640,128]{1,0:T(8,128)(2,1)S(1)}, bf16[640,128]{1,0:T(8,128)(2,1)S(1)}, u32[]{:S(2)}, u32[]{:S(2)}) collective-permute-start(bf16[640,128]{1,0:T(8,128)(2,1)S(1)} %get-tuple-element.82.old_right), channel_id=1, source_target_pairs={{0,2},{1,3},{2,4},{3,5},{4,6},{5,7},{6,8},{7,9},{8,10},{9,11},{10,... | collective-permute-start | bytes 491528 | tf_op jit(solution)/shard_map/ppermute | solution.py:238
  51.3 1.1 %collective-permute-start.23 = (bf16[640,128]{1,0:T(8,128)(2,1)S(1)}, bf16[640,128]{1,0:T(8,128)(2,1)S(1)}, u32[]{:S(2)}, u32[]{:S(2)}) collective-permute-start(bf16[640,128]{1,0:T(8,128)(2,1)S(1)} %get-tuple-element.87.old_upper), channel_id=1, source_target_pairs={{0,16},{16,0},{1,17},{17,1},{2,18},{18,2},{3,19},{19,3},{4,20},{20... | collective-permute-start | bytes 491528 | tf_op jit(solution)/shard_map/ppermute | solution.py:241
  53.1 2.7 %collective-permute-done.20.upper_in = bf16[640,128]{1,0:T(8,128)(2,1)S(1)} collective-permute-done((bf16[640,128]{1,0:T(8,128)(2,1)S(1)}, bf16[640,128]{1,0:T(8,128)(2,1)S(1)}, u32[]{:S(2)}, u32[]{:S(2)}) %collective-permute-start.20) | collective-permute-done | bytes 163872 | tf_op jit(solution)/shard_map/ppermute | solution.py:241
  57.4 1.9 %collective-permute-done.17.upper_in = bf16[640,128]{1,0:T(8,128)(2,1)S(1)} collective-permute-done((bf16[640,128]{1,0:T(8,128)(2,1)S(1)}, bf16[640,128]{1,0:T(8,128)(2,1)S(1)}, u32[]{:S(2)}, u32[]{:S(2)}) %collective-permute-start.17) | collective-permute-done | bytes 163872 | tf_op jit(solution)/shard_map/ppermute | solution.py:241
  62.7 2.7 %collective-permute-start.24 = (bf16[640,128]{1,0:T(8,128)(2,1)S(1)}, bf16[640,128]{1,0:T(8,128)(2,1)S(1)}, u32[]{:S(2)}, u32[]{:S(2)}) collective-permute-start(bf16[640,128]{1,0:T(8,128)(2,1)S(1)} %get-tuple-element.91), channel_id=1, source_target_pairs={{0,2},{1,3},{2,4},{3,5},{4,6},{5,7},{6,8},{7,9},{8,10},{9,11},{10,... | collective-permute-start | bytes 491528 | tf_op jit(solution)/shard_map/ppermute | solution.py:238
  65.5 2.2 %collective-permute-start.22 = (bf16[640,256]{1,0:T(8,128)(2,1)S(1)}, bf16[640,256]{1,0:T(8,128)(2,1)S(1)}, u32[]{:S(2)}, u32[]{:S(2)}) collective-permute-start(bf16[640,256]{1,0:T(8,128)(2,1)S(1)} %shard_map.49), channel_id=1, source_target_pairs={{0,16},{16,0},{1,17},{17,1},{2,18},{18,2},{3,19},{19,3},{4,20},{20... | collective-permute-start | bytes 983048 | tf_op jit(solution)/shard_map/ppermute | solution.py:241
  67.7 2.4 %collective-permute-done.25.right_in = bf16[640,128]{1,0:T(8,128)(2,1)S(1)} collective-permute-done((bf16[640,128]{1,0:T(8,128)(2,1)S(1)}, bf16[640,128]{1,0:T(8,128)(2,1)S(1)}, u32[]{:S(2)}, u32[]{:S(2)}) %collective-permute-start.25) | collective-permute-done | bytes 163872 | tf_op jit(solution)/shard_map/ppermute | solution.py:238
  70.9 1.4 %collective-permute-done.27.got = bf16[640,128]{1,0:T(8,128)(2,1)S(1)} collective-permute-done((bf16[640,128]{1,0:T(8,128)(2,1)S(1)}, bf16[640,128]{1,0:T(8,128)(2,1)S(1)}, u32[]{:S(2)}, u32[]{:S(2)}) %collective-permute-start.27) | collective-permute-done | bytes 163872 | tf_op jit(solution)/shard_map/ppermute | solution.py:235
  72.3 2.8 %collective-permute-done.22.upper_in = bf16[640,256]{1,0:T(8,128)(2,1)S(1)} collective-permute-done((bf16[640,256]{1,0:T(8,128)(2,1)S(1)}, bf16[640,256]{1,0:T(8,128)(2,1)S(1)}, u32[]{:S(2)}, u32[]{:S(2)}) %collective-permute-start.22) | collective-permute-done | bytes 327712 | tf_op jit(solution)/shard_map/ppermute | solution.py:241
  75.8 1.4 %last.1 = bf16[1280,256]{1,0:T(8,128)(2,1)} custom-call(bf16[1280,1280]{1,0:T(8,128)(2,1)S(1)} %shard_map.28.own.mapping, f32[1280,256]{1,0:T(8,128)S(1)} %shard_map.50.total, bf16[640,256]{1,0:T(8,128)(2,1)S(1)} %shard_map.54.right_in), custom_call_target="tpu_custom_call" | custom-call | flops 400000000 | bytes 2000000 | tf_op jit(solution)/shard_map/last/pallas_call | solution.py:209
  (61 shorter events, 24.3 us)
Async XLA Ops:
  0.0 16.8 %collective-permute-start = (bf16[1280,1280]{1,0:T(8,128)(2,1)}, bf16[1280,1280]{1,0:T(8,128)(2,1)S(1)}, u32[]{:S(2)}, u32[]{:S(2)}) collective-permute-start(bf16[1280,1280]{1,0:T(8,128)(2,1)} %bitcast.3), channel_id=1, source_target_pairs={{0,1},{1,0},{2,3},{3,2},{4,5},{5,4},{6,7},{7,6},{8,9},{9,8},{10,11... | collective-permute-start | bytes 9830408 | tf_op jit(solution)/shard_map/ppermute | solution.py:235
  0.5 12.3 %collective-permute-start.1 = (bf16[1280,256]{1,0:T(8,128)(2,1)}, bf16[1280,256]{1,0:T(8,128)(2,1)S(1)}, u32[]{:S(2)}, u32[]{:S(2)}) collective-permute-start(bf16[1280,256]{1,0:T(8,128)(2,1)} %bitcast.5), channel_id=1, source_target_pairs={{0,1},{1,0},{2,3},{3,2},{4,5},{5,4},{6,7},{7,6},{8,9},{9,8},{10,11... | collective-permute-start | bytes 1966088 | tf_op jit(solution)/shard_map/ppermute | solution.py:235
  1.7 10.9 %collective-permute-start.3 = (bf16[640,256]{1,0:T(8,128)(2,1)S(1)}, bf16[640,256]{1,0:T(8,128)(2,1)S(1)}, u32[]{:S(2)}, u32[]{:S(2)}) collective-permute-start(bf16[640,256]{1,0:T(8,128)(2,1)S(1)} %get-tuple-element.57), channel_id=1, source_target_pairs={{0,16},{16,0},{1,17},{17,1},{2,18},{18,2},{3,19},{19,3},{4,20},{20... | collective-permute-start | bytes 983048 | tf_op jit(solution)/shard_map/ppermute | solution.py:241
  13.0 9.7 %collective-permute-start.2 = (bf16[640,128]{1,0:T(8,128)(2,1)S(1)}, bf16[640,128]{1,0:T(8,128)(2,1)S(1)}, u32[]{:S(2)}, u32[]{:S(2)}) collective-permute-start(bf16[640,128]{1,0:T(8,128)(2,1)S(1)} %get-tuple-element.52.old_right), channel_id=1, source_target_pairs={{0,2},{1,3},{2,4},{3,5},{4,6},{5,7},{6,8},{7,9},{8,10},{9,11},{10,... | collective-permute-start | bytes 491528 | tf_op jit(solution)/shard_map/ppermute | solution.py:238
  18.0 9.0 %collective-permute-start.7 = (bf16[640,128]{1,0:T(8,128)(2,1)S(1)}, bf16[640,128]{1,0:T(8,128)(2,1)S(1)}, u32[]{:S(2)}, u32[]{:S(2)}) collective-permute-start(bf16[640,128]{1,0:T(8,128)(2,1)S(1)} %get-tuple-element.63.old_right), channel_id=1, source_target_pairs={{0,2},{1,3},{2,4},{3,5},{4,6},{5,7},{6,8},{7,9},{8,10},{9,11},{10,... | collective-permute-start | bytes 491528 | tf_op jit(solution)/shard_map/ppermute | solution.py:238
  19.5 8.1 %collective-permute-start.9 = (bf16[640,128]{1,0:T(8,128)(2,1)S(1)}, bf16[640,128]{1,0:T(8,128)(2,1)S(1)}, u32[]{:S(2)}, u32[]{:S(2)}) collective-permute-start(bf16[640,128]{1,0:T(8,128)(2,1)S(1)} %get-tuple-element.64.old_upper), channel_id=1, source_target_pairs={{0,16},{16,0},{1,17},{17,1},{2,18},{18,2},{3,19},{19,3},{4,20},{20... | collective-permute-start | bytes 491528 | tf_op jit(solution)/shard_map/ppermute | solution.py:241
  24.0 8.7 %collective-permute-start.5 = (bf16[640,128]{1,0:T(8,128)(2,1)S(1)}, bf16[640,128]{1,0:T(8,128)(2,1)S(1)}, u32[]{:S(2)}, u32[]{:S(2)}) collective-permute-start(bf16[640,128]{1,0:T(8,128)(2,1)S(1)} %get-tuple-element.65.old_right), channel_id=1, source_target_pairs={{0,2},{1,3},{2,4},{3,5},{4,6},{5,7},{6,8},{7,9},{8,10},{9,11},{10,... | collective-permute-start | bytes 491528 | tf_op jit(solution)/shard_map/ppermute | solution.py:238
  24.0 9.4 %collective-permute-start.6 = (bf16[640,128]{1,0:T(8,128)(2,1)S(1)}, bf16[640,128]{1,0:T(8,128)(2,1)S(1)}, u32[]{:S(2)}, u32[]{:S(2)}) collective-permute-start(bf16[640,128]{1,0:T(8,128)(2,1)S(1)} %get-tuple-element.66.old_upper), channel_id=1, source_target_pairs={{0,16},{16,0},{1,17},{17,1},{2,18},{18,2},{3,19},{19,3},{4,20},{20... | collective-permute-start | bytes 491528 | tf_op jit(solution)/shard_map/ppermute | solution.py:241
  25.0 9.7 %collective-permute-start.8 = (bf16[640,128]{1,0:T(8,128)(2,1)S(1)}, bf16[640,128]{1,0:T(8,128)(2,1)S(1)}, u32[]{:S(2)}, u32[]{:S(2)}) collective-permute-start(bf16[640,128]{1,0:T(8,128)(2,1)S(1)} %get-tuple-element.71.old_upper), channel_id=1, source_target_pairs={{0,16},{16,0},{1,17},{17,1},{2,18},{18,2},{3,19},{19,3},{4,20},{20... | collective-permute-start | bytes 491528 | tf_op jit(solution)/shard_map/ppermute | solution.py:241
  28.2 9.0 %collective-permute-start.12 = (bf16[640,128]{1,0:T(8,128)(2,1)S(1)}, bf16[640,128]{1,0:T(8,128)(2,1)S(1)}, u32[]{:S(2)}, u32[]{:S(2)}) collective-permute-start(bf16[640,128]{1,0:T(8,128)(2,1)S(1)} %get-tuple-element.72.old_right), channel_id=1, source_target_pairs={{0,2},{1,3},{2,4},{3,5},{4,6},{5,7},{6,8},{7,9},{8,10},{9,11},{10,... | collective-permute-start | bytes 491528 | tf_op jit(solution)/shard_map/ppermute | solution.py:238
  28.5 9.9 %collective-permute-start.13 = (bf16[640,128]{1,0:T(8,128)(2,1)S(1)}, bf16[640,128]{1,0:T(8,128)(2,1)S(1)}, u32[]{:S(2)}, u32[]{:S(2)}) collective-permute-start(bf16[640,128]{1,0:T(8,128)(2,1)S(1)} %get-tuple-element.69.old_upper), channel_id=1, source_target_pairs={{0,16},{16,0},{1,17},{17,1},{2,18},{18,2},{3,19},{19,3},{4,20},{20... | collective-permute-start | bytes 491528 | tf_op jit(solution)/shard_map/ppermute | solution.py:241
  32.7 9.0 %collective-permute-start.15 = (bf16[640,128]{1,0:T(8,128)(2,1)S(1)}, bf16[640,128]{1,0:T(8,128)(2,1)S(1)}, u32[]{:S(2)}, u32[]{:S(2)}) collective-permute-start(bf16[640,128]{1,0:T(8,128)(2,1)S(1)} %get-tuple-element.73.old_upper), channel_id=1, source_target_pairs={{0,16},{16,0},{1,17},{17,1},{2,18},{18,2},{3,19},{19,3},{4,20},{20... | collective-permute-start | bytes 491528 | tf_op jit(solution)/shard_map/ppermute | solution.py:241
  35.3 9.0 %collective-permute-start.10 = (bf16[640,128]{1,0:T(8,128)(2,1)S(1)}, bf16[640,128]{1,0:T(8,128)(2,1)S(1)}, u32[]{:S(2)}, u32[]{:S(2)}) collective-permute-start(bf16[640,128]{1,0:T(8,128)(2,1)S(1)} %get-tuple-element.74.old_right), channel_id=1, source_target_pairs={{0,2},{1,3},{2,4},{3,5},{4,6},{5,7},{6,8},{7,9},{8,10},{9,11},{10,... | collective-permute-start | bytes 491528 | tf_op jit(solution)/shard_map/ppermute | solution.py:238
  36.4 9.1 %collective-permute-start.11 = (bf16[640,128]{1,0:T(8,128)(2,1)S(1)}, bf16[640,128]{1,0:T(8,128)(2,1)S(1)}, u32[]{:S(2)}, u32[]{:S(2)}) collective-permute-start(bf16[640,128]{1,0:T(8,128)(2,1)S(1)} %get-tuple-element.75.old_upper), channel_id=1, source_target_pairs={{0,16},{16,0},{1,17},{17,1},{2,18},{18,2},{3,19},{19,3},{4,20},{20... | collective-permute-start | bytes 491528 | tf_op jit(solution)/shard_map/ppermute | solution.py:241
  37.3 11.5 %collective-permute-start.14 = (bf16[640,128]{1,0:T(8,128)(2,1)S(1)}, bf16[640,128]{1,0:T(8,128)(2,1)S(1)}, u32[]{:S(2)}, u32[]{:S(2)}) collective-permute-start(bf16[640,128]{1,0:T(8,128)(2,1)S(1)} %get-tuple-element.79.old_upper), channel_id=1, source_target_pairs={{0,16},{16,0},{1,17},{17,1},{2,18},{18,2},{3,19},{19,3},{4,20},{20... | collective-permute-start | bytes 491528 | tf_op jit(solution)/shard_map/ppermute | solution.py:241
  42.3 9.0 %collective-permute-start.18 = (bf16[640,128]{1,0:T(8,128)(2,1)S(1)}, bf16[640,128]{1,0:T(8,128)(2,1)S(1)}, u32[]{:S(2)}, u32[]{:S(2)}) collective-permute-start(bf16[640,128]{1,0:T(8,128)(2,1)S(1)} %get-tuple-element.80.old_right), channel_id=1, source_target_pairs={{0,2},{1,3},{2,4},{3,5},{4,6},{5,7},{6,8},{7,9},{8,10},{9,11},{10,... | collective-permute-start | bytes 491528 | tf_op jit(solution)/shard_map/ppermute | solution.py:238
  43.4 9.1 %collective-permute-start.19 = (bf16[640,128]{1,0:T(8,128)(2,1)S(1)}, bf16[640,128]{1,0:T(8,128)(2,1)S(1)}, u32[]{:S(2)}, u32[]{:S(2)}) collective-permute-start(bf16[640,128]{1,0:T(8,128)(2,1)S(1)} %get-tuple-element.77.old_upper), channel_id=1, source_target_pairs={{0,16},{16,0},{1,17},{17,1},{2,18},{18,2},{3,19},{19,3},{4,20},{20... | collective-permute-start | bytes 491528 | tf_op jit(solution)/shard_map/ppermute | solution.py:241
  44.3 11.5 %collective-permute-start.20 = (bf16[640,128]{1,0:T(8,128)(2,1)S(1)}, bf16[640,128]{1,0:T(8,128)(2,1)S(1)}, u32[]{:S(2)}, u32[]{:S(2)}) collective-permute-start(bf16[640,128]{1,0:T(8,128)(2,1)S(1)} %get-tuple-element.81.old_upper), channel_id=1, source_target_pairs={{0,16},{16,0},{1,17},{17,1},{2,18},{18,2},{3,19},{19,3},{4,20},{20... | collective-permute-start | bytes 491528 | tf_op jit(solution)/shard_map/ppermute | solution.py:241
  50.4 8.8 %collective-permute-start.17 = (bf16[640,128]{1,0:T(8,128)(2,1)S(1)}, bf16[640,128]{1,0:T(8,128)(2,1)S(1)}, u32[]{:S(2)}, u32[]{:S(2)}) collective-permute-start(bf16[640,128]{1,0:T(8,128)(2,1)S(1)} %get-tuple-element.83.old_upper), channel_id=1, source_target_pairs={{0,16},{16,0},{1,17},{17,1},{2,18},{18,2},{3,19},{19,3},{4,20},{20... | collective-permute-start | bytes 491528 | tf_op jit(solution)/shard_map/ppermute | solution.py:241
  51.3 10.7 %collective-permute-start.23 = (bf16[640,128]{1,0:T(8,128)(2,1)S(1)}, bf16[640,128]{1,0:T(8,128)(2,1)S(1)}, u32[]{:S(2)}, u32[]{:S(2)}) collective-permute-start(bf16[640,128]{1,0:T(8,128)(2,1)S(1)} %get-tuple-element.87.old_upper), channel_id=1, source_target_pairs={{0,16},{16,0},{1,17},{17,1},{2,18},{18,2},{3,19},{19,3},{4,20},{20... | collective-permute-start | bytes 491528 | tf_op jit(solution)/shard_map/ppermute | solution.py:241
  60.0 10.1 %collective-permute-start.26 = (bf16[640,128]{1,0:T(8,128)(2,1)S(1)}, bf16[640,128]{1,0:T(8,128)(2,1)S(1)}, u32[]{:S(2)}, u32[]{:S(2)}) collective-permute-start(bf16[640,128]{1,0:T(8,128)(2,1)S(1)} %get-tuple-element.85.old_upper), channel_id=1, source_target_pairs={{0,16},{16,0},{1,17},{17,1},{2,18},{18,2},{3,19},{19,3},{4,20},{20... | collective-permute-start | bytes 491528 | tf_op jit(solution)/shard_map/ppermute | solution.py:241
  60.9 9.2 %collective-permute-start.25 = (bf16[640,128]{1,0:T(8,128)(2,1)S(1)}, bf16[640,128]{1,0:T(8,128)(2,1)S(1)}, u32[]{:S(2)}, u32[]{:S(2)}) collective-permute-start(bf16[640,128]{1,0:T(8,128)(2,1)S(1)} %get-tuple-element.90.old_right), channel_id=1, source_target_pairs={{0,2},{1,3},{2,4},{3,5},{4,6},{5,7},{6,8},{7,9},{8,10},{9,11},{10,... | collective-permute-start | bytes 491528 | tf_op jit(solution)/shard_map/ppermute | solution.py:238
  62.7 8.1 %collective-permute-start.24 = (bf16[640,128]{1,0:T(8,128)(2,1)S(1)}, bf16[640,128]{1,0:T(8,128)(2,1)S(1)}, u32[]{:S(2)}, u32[]{:S(2)}) collective-permute-start(bf16[640,128]{1,0:T(8,128)(2,1)S(1)} %get-tuple-element.91), channel_id=1, source_target_pairs={{0,2},{1,3},{2,4},{3,5},{4,6},{5,7},{6,8},{7,9},{8,10},{9,11},{10,... | collective-permute-start | bytes 491528 | tf_op jit(solution)/shard_map/ppermute | solution.py:238
  65.5 9.6 %collective-permute-start.22 = (bf16[640,256]{1,0:T(8,128)(2,1)S(1)}, bf16[640,256]{1,0:T(8,128)(2,1)S(1)}, u32[]{:S(2)}, u32[]{:S(2)}) collective-permute-start(bf16[640,256]{1,0:T(8,128)(2,1)S(1)} %shard_map.49), channel_id=1, source_target_pairs={{0,16},{16,0},{1,17},{17,1},{2,18},{18,2},{3,19},{19,3},{4,20},{20... | collective-permute-start | bytes 983048 | tf_op jit(solution)/shard_map/ppermute | solution.py:241
  (4 other events, 22.8 us)

commit v2 on v1

--- a/solution.py
+++ b/solution.py
@@ -123,7 +123,26 @@
     return jnp.where(lax.axis_index("col") < 2, jnp.zeros_like(right_in), right_in[...])
 
 
-def step_body(first, slot, rows, mapping, right_in, upper_in, source, old_right, old_upper, right, upper):
+def settled_chips(rows):
+    return max(0, (ITERS - 2 - rows) // 2 + 1)
+
+
+def choose_body(rows, left_old, left_new, right_a, left, given):
+    chip = lax.axis_index("col") // 2
+    core = lax.rem(lax.axis_index("col"), 2)
+    settled = chip <= settled_chips(rows)
+    left[...] = jnp.where(settled, left_old[...], left_new[...])
+
+    @pl.when(core == 0)
+    def _():
+        given[...] = right_a[...]
+
+    @pl.when(core == 1)
+    def _():
+        given[...] = left[...]
+
+
+def step_body(first, slot, rows, mapping, right_in, upper_in, source, old_right, old_upper, right, upper=None):
     half = right.shape[0]
     row = lax.axis_index("row")
     time = slot - LAG * row
@@ -131,17 +150,22 @@
 
     @pl.when(jnp.logical_and(active, row == 0))
     def _():
-        total = dot(mapping[:, :half], incoming(first, right_in)) + source[...].astype(jnp.float32)
-        right[...] = total[:half].astype(right.dtype)
-        upper[...] = total[half:].astype(upper.dtype)
-
-    @pl.when(jnp.logical_and(active, jnp.logical_and(row > 0, row == rows - 1)))
+        if upper is None:
+            total = dot(mapping[:half, :half], incoming(first, right_in)) + source[:half, :].astype(jnp.float32)
+            right[...] = total.astype(right.dtype)
+        else:
+            total = dot(mapping[:, :half], incoming(first, right_in)) + source[...].astype(jnp.float32)
+            right[...] = total[:half].astype(right.dtype)
+            upper[...] = total[half:].astype(upper.dtype)
+
+    @pl.when(jnp.logical_and(active, jnp.logical_and(row > 0, jnp.logical_or(row == rows - 1, upper is None))))
     def _():
         total = dot(mapping[:half, :half], incoming(first, right_in)) + dot(mapping[:half, half:], upper_in[...])
         right[...] = (total + source[:half, :].astype(jnp.float32)).astype(right.dtype)
-        upper[...] = old_upper[...]
-
-    if rows > 2:
+        if upper is not None:
+            upper[...] = old_upper[...]
+
+    if rows > 2 and upper is not None:
         @pl.when(jnp.logical_and(active, jnp.logical_and(row > 0, row < rows - 1)))
         def _():
             total = dot(mapping[:, :half], incoming(first, right_in)) + dot(mapping[:, half:], upper_in[...])
@@ -152,7 +176,8 @@
     @pl.when(jnp.logical_not(active))
     def _():
         right[...] = old_right[...]
-        upper[...] = old_upper[...]
+        if upper is not None:
+            upper[...] = old_upper[...]
 
 
 def give_body(first, second, sent):
@@ -182,21 +207,21 @@
         whole[:, width:] = second[...]
 
 
-def begin_body(mapping, upper_in, source, total):
+def begin_body(mapping, right_in, source, total):
+    half = right_in.shape[0]
+    left = jnp.where(lax.axis_index("col") == 0, jnp.zeros_like(right_in), right_in[...])
+    total[...] = dot(mapping[:, :half], left) + source[...].astype(jnp.float32)
+
+
+def last_body(mapping, total, upper_in, out, ready, sems):
     half = upper_in.shape[0]
-    below = jnp.where(lax.axis_index("row") == 0, jnp.zeros_like(upper_in), upper_in[...])
-    total[...] = dot(mapping[:, half:], below) + source[...].astype(jnp.float32)
-
-
-def last_body(mapping, total, right_in, out, ready, sems):
-    half = right_in.shape[0]
     parts = sems.shape[0]
     tall = total.shape[0] // parts
     copies = []
-    left = jnp.where(lax.axis_index("col") == 0, jnp.zeros_like(right_in), right_in[...])
+    below = jnp.where(lax.axis_index("row") == 0, jnp.zeros_like(upper_in), upper_in[...])
     for n in range(parts):
         rows = slice(n * tall, (n + 1) * tall)
-        ready[rows, :] = (total[rows, :] + dot(mapping[rows, :half], left)).astype(ready.dtype)
+        ready[rows, :] = (total[rows, :] + dot(mapping[rows, half:], below)).astype(ready.dtype)
         copy = pltpu.make_async_copy(ready.at[rows, :], out.at[rows, :], sems.at[n])
         copy.start()
         copies.append(copy)
@@ -204,8 +229,8 @@
         copy.wait()
 
 
-def last(mapping, total, right_in, shape):
-    operands = [in_vmem(operand) for operand in (mapping, total, right_in)]
+def last(mapping, total, upper_in, shape):
+    operands = [in_vmem(operand) for operand in (mapping, total, upper_in)]
     return pl.pallas_call(
         last_body,
         out_shape=jax.ShapeDtypeStruct(shape, jnp.bfloat16),
@@ -227,6 +252,9 @@
     count = lax.axis_size("col")
     swap = [(j, j ^ 1) for j in range(count)]
     cross = [(j, (j + 2) % count) for j in range(count)]
+    settled = settled_chips(rows)
+    groups = (range(2 * settled), range(2 * settled, count))
+    settled_apart = [(j, group.start + (j + 2 - group.start) % len(group)) for group in groups for j in group]
     up = [(i, (i + 1) % rows) for i in range(rows)]
     slots = ITERS - 1 + LAG * (rows - 1)
     last_message = ITERS - 2 + LAG * (rows - 2)
@@ -235,7 +263,7 @@
         return lax.ppermute(array, "col", swap)
 
     def rightward(array, wrap=True):
-        return lax.ppermute(array, "col", cross if wrap else cross[:-2])
+        return lax.ppermute(array, "col", cross if wrap else settled_apart)
 
     def upward(array):
         return lax.ppermute(array, "row", up)
@@ -253,7 +281,8 @@
 
     def advance(column, slot, *operands):
         body = functools.partial(step_body, column == "a", slot, rows)
-        return call(body, [trace] * 2, *operands)
+        outs = call(body, [trace] * (1 if slot == slots - 1 else 2), *operands)
+        return outs if len(outs) == 2 else (outs[0], None)
 
     zero = jnp.zeros(trace, jnp.bfloat16)
     below_a, below_b = [None], [None]
@@ -275,13 +304,13 @@
             given, = call(give_body, [trace], upper_b, upper_a)
             whole, = call(join_body, [(half, width)], upper_a, upper_b, exchange(given))
             below_last = upward(whole)
-        right_b, left = new_right_b, new_left
-
-    given, = call(give_body, [trace], right_a, left)
+        right_b, left_old, left = new_right_b, left, new_left
+
+    left, given = call(functools.partial(choose_body, rows), [trace] * 2, left_old, left, right_a)
     got = exchange(given)
-    total, = call(begin_body, [((order, width), jnp.float32)], map_own, below_last, source_own)
     right_in, = call(join_body, [(half, width)], left, right_a, got)
-    out = last(map_own, total, right_in, (order, width))
+    total, = call(begin_body, [((order, width), jnp.float32)], map_own, right_in, source_own)
+    out = last(map_own, total, below_last, (order, width))
     return out[None, None]
 
 

time: 77.6 us -> 75.4 us (0.972)
  starting transfers between devices: 28.3 us -> 26.4 us
  Pallas kernels: 16.1 us -> 14.8 us
  waiting for transfers between devices: 32.6 us -> 33.6 us
    ppermute x9, waiting for transfers between devices: 9.99 us -> 13.1 us  [rightward(): return lax.ppermute(array, 'col', cross if wrap else settled_apart)]
    ppermute x14, waiting for transfers between devices: 21.2 us -> 19 us  [upward(): return lax.ppermute(array, 'row', up)]
    ppermute x9, starting transfers between devices: 10.7 us -> 8.88 us  [rightward(): return lax.ppermute(array, 'col', cross if wrap else settled_apart)]
    pallas_call x25, Pallas kernels: 11.5 us -> 10.2 us  [call(): pl.pallas_call(body, out_shape=[pltpu.VMEM(*(out if isinstance(out[0], tu...]
where the time goes in v2:
time: 75.4 us; the launch traced here: 75.2 us
  waiting for transfers between devices  33.6 us (45%)
  starting transfers between devices  26.4 us (35%)
  Pallas kernels  14.8 us (20%)
    ppermute x14, waiting for transfers between devices, upward(): return lax.ppermute(array, 'row', up)  19 us
    ppermute x14, starting transfers between devices, upward(): return lax.ppermute(array, 'row', up)  16.8 us
    ppermute x9, waiting for transfers between devices, rightward(): return lax.ppermute(array, 'col', cross if wrap else settled_apart)  13.1 us
    pallas_call x25, Pallas kernels, call(): pl.pallas_call(body, out_shape=[pltpu.VMEM(*(out if isinstance(out[0], tu...  10.2 us
    ppermute x9, starting transfers between devices, rightward(): return lax.ppermute(array, 'col', cross if wrap else settled_apart)  8.88 us
    pallas_call x2, Pallas kernels, fetch(): pl.pallas_call(body, out_shape=[pltpu.VMEM(shape, operand.dtype) for shap...  3.14 us
  transfers between devices with their start and end apart: 28, of which 13 were waited for; matrix products, arithmetic and copies ran while one was open for 0% of the time, Pallas kernels for 18%

profile of v2, /device:TPU:0, one launch (start us, length us, event | category | flops | bytes accessed | tf_op | source)
XLA Modules:
  0.0 75.2 jit_solution(4039235144042811143)
XLA Ops:
  0.5 1.2 %shard_map.30 = (bf16[640,256]{1,0:T(8,128)(2,1)S(1)}, bf16[1280,256]{1,0:T(8,128)(2,1)S(1)}) custom-call(bf16[1280,256]{1,0:T(8,128)(2,1)} %bitcast.6), custom_call_target="tpu_custom_call" | custom-call | flops 400000000 | bytes 2000000 | tf_op jit(solution)/shard_map/pallas_call | solution.py:40
  1.7 3.0 %collective-permute-start.3 = (bf16[640,256]{1,0:T(8,128)(2,1)S(1)}, bf16[640,256]{1,0:T(8,128)(2,1)S(1)}, u32[]{:S(2)}, u32[]{:S(2)}) collective-permute-start(bf16[640,256]{1,0:T(8,128)(2,1)S(1)} %get-tuple-element.57), channel_id=1, source_target_pairs={{0,16},{16,0},{1,17},{17,1},{2,18},{18,2},{3,19},{19,3},{4,20},{20... | collective-permute-start | bytes 983048 | tf_op jit(solution)/shard_map/ppermute | solution.py:269
  4.8 7.9 %collective-permute-done.3.whole = bf16[640,256]{1,0:T(8,128)(2,1)S(1)} collective-permute-done((bf16[640,256]{1,0:T(8,128)(2,1)S(1)}, bf16[640,256]{1,0:T(8,128)(2,1)S(1)}, u32[]{:S(2)}, u32[]{:S(2)}) %collective-permute-start.3) | collective-permute-done | bytes 327712 | tf_op jit(solution)/shard_map/ppermute | solution.py:269
  13.0 1.8 %collective-permute-start.5 = (bf16[640,128]{1,0:T(8,128)(2,1)S(1)}, bf16[640,128]{1,0:T(8,128)(2,1)S(1)}, u32[]{:S(2)}, u32[]{:S(2)}) collective-permute-start(bf16[640,128]{1,0:T(8,128)(2,1)S(1)} %get-tuple-element.54.old_right), channel_id=1, source_target_pairs={{0,2},{1,3},{2,4},{3,5},{4,6},{5,7},{6,8},{7,9},{8,10},{9,11},{10,... | collective-permute-start | bytes 491528 | tf_op jit(solution)/shard_map/ppermute | solution.py:266
  14.9 1.9 %shard_map.28.own.mapping = bf16[1280,1280]{1,0:T(8,128)(2,1)S(1)} custom-call(bf16[1280,1280]{1,0:T(8,128)(2,1)} %bitcast.4), custom_call_target="tpu_custom_call" | custom-call | flops 400000000 | bytes 2000000 | tf_op jit(solution)/shard_map/pallas_call | solution.py:40
  18.0 1.6 %collective-permute-start.2 = (bf16[640,128]{1,0:T(8,128)(2,1)S(1)}, bf16[640,128]{1,0:T(8,128)(2,1)S(1)}, u32[]{:S(2)}, u32[]{:S(2)}) collective-permute-start(bf16[640,128]{1,0:T(8,128)(2,1)S(1)} %get-tuple-element.56.old_right), channel_id=1, source_target_pairs={{0,2},{1,3},{2,4},{3,5},{4,6},{5,7},{6,8},{7,9},{8,10},{9,11},{10,... | collective-permute-start | bytes 491528 | tf_op jit(solution)/shard_map/ppermute | solution.py:266
  20.5 2.3 %collective-permute-done.5.right_in = bf16[640,128]{1,0:T(8,128)(2,1)S(1)} collective-permute-done((bf16[640,128]{1,0:T(8,128)(2,1)S(1)}, bf16[640,128]{1,0:T(8,128)(2,1)S(1)}, u32[]{:S(2)}, u32[]{:S(2)}) %collective-permute-start.5) | collective-permute-done | bytes 163872 | tf_op jit(solution)/shard_map/ppermute | solution.py:266
  25.0 1.1 %collective-permute-start.12 = (bf16[640,128]{1,0:T(8,128)(2,1)S(1)}, bf16[640,128]{1,0:T(8,128)(2,1)S(1)}, u32[]{:S(2)}, u32[]{:S(2)}) collective-permute-start(bf16[640,128]{1,0:T(8,128)(2,1)S(1)} %get-tuple-element.69.old_upper), channel_id=1, source_target_pairs={{0,16},{16,0},{1,17},{17,1},{2,18},{18,2},{3,19},{19,3},{4,20},{20... | collective-permute-start | bytes 491528 | tf_op jit(solution)/shard_map/ppermute | solution.py:269
  29.3 3.4 %collective-permute-done.9.right_in = bf16[640,128]{1,0:T(8,128)(2,1)S(1)} collective-permute-done((bf16[640,128]{1,0:T(8,128)(2,1)S(1)}, bf16[640,128]{1,0:T(8,128)(2,1)S(1)}, u32[]{:S(2)}, u32[]{:S(2)}) %collective-permute-start.9) | collective-permute-done | bytes 163872 | tf_op jit(solution)/shard_map/ppermute | solution.py:266
  35.3 1.1 %collective-permute-start.15 = (bf16[640,128]{1,0:T(8,128)(2,1)S(1)}, bf16[640,128]{1,0:T(8,128)(2,1)S(1)}, u32[]{:S(2)}, u32[]{:S(2)}) collective-permute-start(bf16[640,128]{1,0:T(8,128)(2,1)S(1)} %get-tuple-element.76.old_right), channel_id=1, source_target_pairs={{0,2},{1,3},{2,4},{3,5},{4,6},{5,7},{6,8},{7,9},{8,10},{9,11},{10,... | collective-permute-start | bytes 491528 | tf_op jit(solution)/shard_map/ppermute | solution.py:266
  37.3 1.1 %collective-permute-start.18 = (bf16[640,128]{1,0:T(8,128)(2,1)S(1)}, bf16[640,128]{1,0:T(8,128)(2,1)S(1)}, u32[]{:S(2)}, u32[]{:S(2)}) collective-permute-start(bf16[640,128]{1,0:T(8,128)(2,1)S(1)} %get-tuple-element.77.old_upper), channel_id=1, source_target_pairs={{0,16},{16,0},{1,17},{17,1},{2,18},{18,2},{3,19},{19,3},{4,20},{20... | collective-permute-start | bytes 491528 | tf_op jit(solution)/shard_map/ppermute | solution.py:269
  39.0 2.7 %collective-permute-done.11.upper_in = bf16[640,128]{1,0:T(8,128)(2,1)S(1)} collective-permute-done((bf16[640,128]{1,0:T(8,128)(2,1)S(1)}, bf16[640,128]{1,0:T(8,128)(2,1)S(1)}, u32[]{:S(2)}, u32[]{:S(2)}) %collective-permute-start.11) | collective-permute-done | bytes 163872 | tf_op jit(solution)/shard_map/ppermute | solution.py:269
  42.3 1.1 %collective-permute-start.13 = (bf16[640,128]{1,0:T(8,128)(2,1)S(1)}, bf16[640,128]{1,0:T(8,128)(2,1)S(1)}, u32[]{:S(2)}, u32[]{:S(2)}) collective-permute-start(bf16[640,128]{1,0:T(8,128)(2,1)S(1)} %get-tuple-element.78.old_right), channel_id=1, source_target_pairs={{0,2},{1,3},{2,4},{3,5},{4,6},{5,7},{6,8},{7,9},{8,10},{9,11},{10,... | collective-permute-start | bytes 491528 | tf_op jit(solution)/shard_map/ppermute | solution.py:266
  44.3 1.1 %collective-permute-start.17 = (bf16[640,128]{1,0:T(8,128)(2,1)S(1)}, bf16[640,128]{1,0:T(8,128)(2,1)S(1)}, u32[]{:S(2)}, u32[]{:S(2)}) collective-permute-start(bf16[640,128]{1,0:T(8,128)(2,1)S(1)} %get-tuple-element.83.old_upper), channel_id=1, source_target_pairs={{0,16},{16,0},{1,17},{17,1},{2,18},{18,2},{3,19},{19,3},{4,20},{20... | collective-permute-start | bytes 491528 | tf_op jit(solution)/shard_map/ppermute | solution.py:269
  46.0 2.7 %collective-permute-done.18.upper_in = bf16[640,128]{1,0:T(8,128)(2,1)S(1)} collective-permute-done((bf16[640,128]{1,0:T(8,128)(2,1)S(1)}, bf16[640,128]{1,0:T(8,128)(2,1)S(1)}, u32[]{:S(2)}, u32[]{:S(2)}) %collective-permute-start.18) | collective-permute-done | bytes 163872 | tf_op jit(solution)/shard_map/ppermute | solution.py:269
  49.3 1.1 %collective-permute-start.20 = (bf16[640,128]{1,0:T(8,128)(2,1)S(1)}, bf16[640,128]{1,0:T(8,128)(2,1)S(1)}, u32[]{:S(2)}, u32[]{:S(2)}) collective-permute-start(bf16[640,128]{1,0:T(8,128)(2,1)S(1)} %get-tuple-element.84.old_right), channel_id=1, source_target_pairs={{0,2},{1,3},{2,4},{3,5},{4,6},{5,7},{6,8},{7,9},{8,10},{9,11},{10,... | collective-permute-start | bytes 491528 | tf_op jit(solution)/shard_map/ppermute | solution.py:266
  51.3 1.1 %collective-permute-start.22 = (bf16[640,128]{1,0:T(8,128)(2,1)S(1)}, bf16[640,128]{1,0:T(8,128)(2,1)S(1)}, u32[]{:S(2)}, u32[]{:S(2)}) collective-permute-start(bf16[640,128]{1,0:T(8,128)(2,1)S(1)} %get-tuple-element.85.old_upper), channel_id=1, source_target_pairs={{0,16},{16,0},{1,17},{17,1},{2,18},{18,2},{3,19},{19,3},{4,20},{20... | collective-permute-start | bytes 491528 | tf_op jit(solution)/shard_map/ppermute | solution.py:269
  53.1 2.7 %collective-permute-done.17.upper_in = bf16[640,128]{1,0:T(8,128)(2,1)S(1)} collective-permute-done((bf16[640,128]{1,0:T(8,128)(2,1)S(1)}, bf16[640,128]{1,0:T(8,128)(2,1)S(1)}, u32[]{:S(2)}, u32[]{:S(2)}) %collective-permute-start.17) | collective-permute-done | bytes 163872 | tf_op jit(solution)/shard_map/ppermute | solution.py:269
  57.4 1.9 %collective-permute-done.21.upper_in = bf16[640,128]{1,0:T(8,128)(2,1)S(1)} collective-permute-done((bf16[640,128]{1,0:T(8,128)(2,1)S(1)}, bf16[640,128]{1,0:T(8,128)(2,1)S(1)}, u32[]{:S(2)}, u32[]{:S(2)}) %collective-permute-start.21) | collective-permute-done | bytes 163872 | tf_op jit(solution)/shard_map/ppermute | solution.py:269
  60.9 1.0 %collective-permute-start.19 = (bf16[640,128]{1,0:T(8,128)(2,1)S(1)}, bf16[640,128]{1,0:T(8,128)(2,1)S(1)}, u32[]{:S(2)}, u32[]{:S(2)}) collective-permute-start(bf16[640,128]{1,0:T(8,128)(2,1)S(1)} %get-tuple-element.86.old_right), channel_id=1, source_target_pairs={{0,2},{1,3},{2,4},{3,5},{4,6},{5,7},{6,8},{7,9},{8,10},{9,11},{10,... | collective-permute-start | bytes 491528 | tf_op jit(solution)/shard_map/ppermute | solution.py:266
  62.9 2.2 %collective-permute-start.27 = (bf16[640,256]{1,0:T(8,128)(2,1)S(1)}, bf16[640,256]{1,0:T(8,128)(2,1)S(1)}, u32[]{:S(2)}, u32[]{:S(2)}) collective-permute-start(bf16[640,256]{1,0:T(8,128)(2,1)S(1)} %shard_map.54), channel_id=1, source_target_pairs={{0,16},{16,0},{1,17},{17,1},{2,18},{18,2},{3,19},{19,3},{4,20},{20... | collective-permute-start | bytes 983048 | tf_op jit(solution)/shard_map/ppermute | solution.py:269
  65.1 5.6 %collective-permute-done.19.right_in.left_old = bf16[640,128]{1,0:T(8,128)(2,1)S(1)} collective-permute-done((bf16[640,128]{1,0:T(8,128)(2,1)S(1)}, bf16[640,128]{1,0:T(8,128)(2,1)S(1)}, u32[]{:S(2)}, u32[]{:S(2)}) %collective-permute-start.19) | collective-permute-done | bytes 163872 | tf_op jit(solution)/shard_map/ppermute | solution.py:266
  70.9 1.4 %collective-permute-done.25.got = bf16[640,128]{1,0:T(8,128)(2,1)S(1)} collective-permute-done((bf16[640,128]{1,0:T(8,128)(2,1)S(1)}, bf16[640,128]{1,0:T(8,128)(2,1)S(1)}, u32[]{:S(2)}, u32[]{:S(2)}) %collective-permute-start.25) | collective-permute-done | bytes 163872 | tf_op jit(solution)/shard_map/ppermute | solution.py:263
  73.6 1.4 %last.1 = bf16[1280,256]{1,0:T(8,128)(2,1)} custom-call(bf16[1280,1280]{1,0:T(8,128)(2,1)S(1)} %shard_map.28.own.mapping, f32[1280,256]{1,0:T(8,128)S(1)} %shard_map.52.total, bf16[640,256]{1,0:T(8,128)(2,1)S(1)} %collective-permute-done.27.upper_in), custom_call_target="tpu_custom_call" | custom-call | flops 400000000 | bytes 2000000 | tf_op jit(solution)/shard_map/last/pallas_call | solution.py:234
  (61 shorter events, 22.3 us)
Async XLA Ops:
  0.0 16.8 %collective-permute-start = (bf16[1280,1280]{1,0:T(8,128)(2,1)}, bf16[1280,1280]{1,0:T(8,128)(2,1)S(1)}, u32[]{:S(2)}, u32[]{:S(2)}) collective-permute-start(bf16[1280,1280]{1,0:T(8,128)(2,1)} %bitcast.3), channel_id=1, source_target_pairs={{0,1},{1,0},{2,3},{3,2},{4,5},{5,4},{6,7},{7,6},{8,9},{9,8},{10,11... | collective-permute-start | bytes 9830408 | tf_op jit(solution)/shard_map/ppermute | solution.py:263
  0.5 12.3 %collective-permute-start.1 = (bf16[1280,256]{1,0:T(8,128)(2,1)}, bf16[1280,256]{1,0:T(8,128)(2,1)S(1)}, u32[]{:S(2)}, u32[]{:S(2)}) collective-permute-start(bf16[1280,256]{1,0:T(8,128)(2,1)} %bitcast.5), channel_id=1, source_target_pairs={{0,1},{1,0},{2,3},{3,2},{4,5},{5,4},{6,7},{7,6},{8,9},{9,8},{10,11... | collective-permute-start | bytes 1966088 | tf_op jit(solution)/shard_map/ppermute | solution.py:263
  1.7 10.9 %collective-permute-start.3 = (bf16[640,256]{1,0:T(8,128)(2,1)S(1)}, bf16[640,256]{1,0:T(8,128)(2,1)S(1)}, u32[]{:S(2)}, u32[]{:S(2)}) collective-permute-start(bf16[640,256]{1,0:T(8,128)(2,1)S(1)} %get-tuple-element.57), channel_id=1, source_target_pairs={{0,16},{16,0},{1,17},{17,1},{2,18},{18,2},{3,19},{19,3},{4,20},{20... | collective-permute-start | bytes 983048 | tf_op jit(solution)/shard_map/ppermute | solution.py:269
  13.0 9.7 %collective-permute-start.5 = (bf16[640,128]{1,0:T(8,128)(2,1)S(1)}, bf16[640,128]{1,0:T(8,128)(2,1)S(1)}, u32[]{:S(2)}, u32[]{:S(2)}) collective-permute-start(bf16[640,128]{1,0:T(8,128)(2,1)S(1)} %get-tuple-element.54.old_right), channel_id=1, source_target_pairs={{0,2},{1,3},{2,4},{3,5},{4,6},{5,7},{6,8},{7,9},{8,10},{9,11},{10,... | collective-permute-start | bytes 491528 | tf_op jit(solution)/shard_map/ppermute | solution.py:266
  18.0 9.0 %collective-permute-start.2 = (bf16[640,128]{1,0:T(8,128)(2,1)S(1)}, bf16[640,128]{1,0:T(8,128)(2,1)S(1)}, u32[]{:S(2)}, u32[]{:S(2)}) collective-permute-start(bf16[640,128]{1,0:T(8,128)(2,1)S(1)} %get-tuple-element.56.old_right), channel_id=1, source_target_pairs={{0,2},{1,3},{2,4},{3,5},{4,6},{5,7},{6,8},{7,9},{8,10},{9,11},{10,... | collective-permute-start | bytes 491528 | tf_op jit(solution)/shard_map/ppermute | solution.py:266
  19.5 8.1 %collective-permute-start.6 = (bf16[640,128]{1,0:T(8,128)(2,1)S(1)}, bf16[640,128]{1,0:T(8,128)(2,1)S(1)}, u32[]{:S(2)}, u32[]{:S(2)}) collective-permute-start(bf16[640,128]{1,0:T(8,128)(2,1)S(1)} %get-tuple-element.66.old_upper), channel_id=1, source_target_pairs={{0,16},{16,0},{1,17},{17,1},{2,18},{18,2},{3,19},{19,3},{4,20},{20... | collective-permute-start | bytes 491528 | tf_op jit(solution)/shard_map/ppermute | solution.py:269
  24.0 8.7 %collective-permute-start.9 = (bf16[640,128]{1,0:T(8,128)(2,1)S(1)}, bf16[640,128]{1,0:T(8,128)(2,1)S(1)}, u32[]{:S(2)}, u32[]{:S(2)}) collective-permute-start(bf16[640,128]{1,0:T(8,128)(2,1)S(1)} %get-tuple-element.68.old_right), channel_id=1, source_target_pairs={{0,2},{1,3},{2,4},{3,5},{4,6},{5,7},{6,8},{7,9},{8,10},{9,11},{10,... | collective-permute-start | bytes 491528 | tf_op jit(solution)/shard_map/ppermute | solution.py:266
  24.0 9.4 %collective-permute-start.10 = (bf16[640,128]{1,0:T(8,128)(2,1)S(1)}, bf16[640,128]{1,0:T(8,128)(2,1)S(1)}, u32[]{:S(2)}, u32[]{:S(2)}) collective-permute-start(bf16[640,128]{1,0:T(8,128)(2,1)S(1)} %get-tuple-element.64.old_upper), channel_id=1, source_target_pairs={{0,16},{16,0},{1,17},{17,1},{2,18},{18,2},{3,19},{19,3},{4,20},{20... | collective-permute-start | bytes 491528 | tf_op jit(solution)/shard_map/ppermute | solution.py:269
  25.0 9.7 %collective-permute-start.12 = (bf16[640,128]{1,0:T(8,128)(2,1)S(1)}, bf16[640,128]{1,0:T(8,128)(2,1)S(1)}, u32[]{:S(2)}, u32[]{:S(2)}) collective-permute-start(bf16[640,128]{1,0:T(8,128)(2,1)S(1)} %get-tuple-element.69.old_upper), channel_id=1, source_target_pairs={{0,16},{16,0},{1,17},{17,1},{2,18},{18,2},{3,19},{19,3},{4,20},{20... | collective-permute-start | bytes 491528 | tf_op jit(solution)/shard_map/ppermute | solution.py:269
  28.2 9.0 %collective-permute-start.7 = (bf16[640,128]{1,0:T(8,128)(2,1)S(1)}, bf16[640,128]{1,0:T(8,128)(2,1)S(1)}, u32[]{:S(2)}, u32[]{:S(2)}) collective-permute-start(bf16[640,128]{1,0:T(8,128)(2,1)S(1)} %get-tuple-element.70.old_right), channel_id=1, source_target_pairs={{0,2},{1,3},{2,4},{3,5},{4,6},{5,7},{6,8},{7,9},{8,10},{9,11},{10,... | collective-permute-start | bytes 491528 | tf_op jit(solution)/shard_map/ppermute | solution.py:266
  28.5 9.9 %collective-permute-start.8 = (bf16[640,128]{1,0:T(8,128)(2,1)S(1)}, bf16[640,128]{1,0:T(8,128)(2,1)S(1)}, u32[]{:S(2)}, u32[]{:S(2)}) collective-permute-start(bf16[640,128]{1,0:T(8,128)(2,1)S(1)} %get-tuple-element.71.old_upper), channel_id=1, source_target_pairs={{0,16},{16,0},{1,17},{17,1},{2,18},{18,2},{3,19},{19,3},{4,20},{20... | collective-permute-start | bytes 491528 | tf_op jit(solution)/shard_map/ppermute | solution.py:269
  32.7 9.0 %collective-permute-start.11 = (bf16[640,128]{1,0:T(8,128)(2,1)S(1)}, bf16[640,128]{1,0:T(8,128)(2,1)S(1)}, u32[]{:S(2)}, u32[]{:S(2)}) collective-permute-start(bf16[640,128]{1,0:T(8,128)(2,1)S(1)} %get-tuple-element.75.old_upper), channel_id=1, source_target_pairs={{0,16},{16,0},{1,17},{17,1},{2,18},{18,2},{3,19},{19,3},{4,20},{20... | collective-permute-start | bytes 491528 | tf_op jit(solution)/shard_map/ppermute | solution.py:269
  35.3 9.0 %collective-permute-start.15 = (bf16[640,128]{1,0:T(8,128)(2,1)S(1)}, bf16[640,128]{1,0:T(8,128)(2,1)S(1)}, u32[]{:S(2)}, u32[]{:S(2)}) collective-permute-start(bf16[640,128]{1,0:T(8,128)(2,1)S(1)} %get-tuple-element.76.old_right), channel_id=1, source_target_pairs={{0,2},{1,3},{2,4},{3,5},{4,6},{5,7},{6,8},{7,9},{8,10},{9,11},{10,... | collective-permute-start | bytes 491528 | tf_op jit(solution)/shard_map/ppermute | solution.py:266
  36.4 9.1 %collective-permute-start.16 = (bf16[640,128]{1,0:T(8,128)(2,1)S(1)}, bf16[640,128]{1,0:T(8,128)(2,1)S(1)}, u32[]{:S(2)}, u32[]{:S(2)}) collective-permute-start(bf16[640,128]{1,0:T(8,128)(2,1)S(1)} %get-tuple-element.73.old_upper), channel_id=1, source_target_pairs={{0,16},{16,0},{1,17},{17,1},{2,18},{18,2},{3,19},{19,3},{4,20},{20... | collective-permute-start | bytes 491528 | tf_op jit(solution)/shard_map/ppermute | solution.py:269
  37.3 11.5 %collective-permute-start.18 = (bf16[640,128]{1,0:T(8,128)(2,1)S(1)}, bf16[640,128]{1,0:T(8,128)(2,1)S(1)}, u32[]{:S(2)}, u32[]{:S(2)}) collective-permute-start(bf16[640,128]{1,0:T(8,128)(2,1)S(1)} %get-tuple-element.77.old_upper), channel_id=1, source_target_pairs={{0,16},{16,0},{1,17},{17,1},{2,18},{18,2},{3,19},{19,3},{4,20},{20... | collective-permute-start | bytes 491528 | tf_op jit(solution)/shard_map/ppermute | solution.py:269
  42.3 9.0 %collective-permute-start.13 = (bf16[640,128]{1,0:T(8,128)(2,1)S(1)}, bf16[640,128]{1,0:T(8,128)(2,1)S(1)}, u32[]{:S(2)}, u32[]{:S(2)}) collective-permute-start(bf16[640,128]{1,0:T(8,128)(2,1)S(1)} %get-tuple-element.78.old_right), channel_id=1, source_target_pairs={{0,2},{1,3},{2,4},{3,5},{4,6},{5,7},{6,8},{7,9},{8,10},{9,11},{10,... | collective-permute-start | bytes 491528 | tf_op jit(solution)/shard_map/ppermute | solution.py:266
  43.4 9.1 %collective-permute-start.14 = (bf16[640,128]{1,0:T(8,128)(2,1)S(1)}, bf16[640,128]{1,0:T(8,128)(2,1)S(1)}, u32[]{:S(2)}, u32[]{:S(2)}) collective-permute-start(bf16[640,128]{1,0:T(8,128)(2,1)S(1)} %get-tuple-element.79.old_upper), channel_id=1, source_target_pairs={{0,16},{16,0},{1,17},{17,1},{2,18},{18,2},{3,19},{19,3},{4,20},{20... | collective-permute-start | bytes 491528 | tf_op jit(solution)/shard_map/ppermute | solution.py:269
  44.3 11.5 %collective-permute-start.17 = (bf16[640,128]{1,0:T(8,128)(2,1)S(1)}, bf16[640,128]{1,0:T(8,128)(2,1)S(1)}, u32[]{:S(2)}, u32[]{:S(2)}) collective-permute-start(bf16[640,128]{1,0:T(8,128)(2,1)S(1)} %get-tuple-element.83.old_upper), channel_id=1, source_target_pairs={{0,16},{16,0},{1,17},{17,1},{2,18},{18,2},{3,19},{19,3},{4,20},{20... | collective-permute-start | bytes 491528 | tf_op jit(solution)/shard_map/ppermute | solution.py:269
  50.4 8.8 %collective-permute-start.21 = (bf16[640,128]{1,0:T(8,128)(2,1)S(1)}, bf16[640,128]{1,0:T(8,128)(2,1)S(1)}, u32[]{:S(2)}, u32[]{:S(2)}) collective-permute-start(bf16[640,128]{1,0:T(8,128)(2,1)S(1)} %get-tuple-element.81.old_upper), channel_id=1, source_target_pairs={{0,16},{16,0},{1,17},{17,1},{2,18},{18,2},{3,19},{19,3},{4,20},{20... | collective-permute-start | bytes 491528 | tf_op jit(solution)/shard_map/ppermute | solution.py:269
  51.3 10.7 %collective-permute-start.22 = (bf16[640,128]{1,0:T(8,128)(2,1)S(1)}, bf16[640,128]{1,0:T(8,128)(2,1)S(1)}, u32[]{:S(2)}, u32[]{:S(2)}) collective-permute-start(bf16[640,128]{1,0:T(8,128)(2,1)S(1)} %get-tuple-element.85.old_upper), channel_id=1, source_target_pairs={{0,16},{16,0},{1,17},{17,1},{2,18},{18,2},{3,19},{19,3},{4,20},{20... | collective-permute-start | bytes 491528 | tf_op jit(solution)/shard_map/ppermute | solution.py:269
  60.0 10.7 %collective-permute-start.24 = (bf16[640,128]{1,0:T(8,128)(2,1)S(1)}, bf16[640,128]{1,0:T(8,128)(2,1)S(1)}, u32[]{:S(2)}, u32[]{:S(2)}) collective-permute-start(bf16[640,128]{1,0:T(8,128)(2,1)S(1)} %get-tuple-element.87.old_upper), channel_id=1, source_target_pairs={{0,16},{16,0},{1,17},{17,1},{2,18},{18,2},{3,19},{19,3},{4,20},{20... | collective-permute-start | bytes 491528 | tf_op jit(solution)/shard_map/ppermute | solution.py:269
  60.9 9.8 %collective-permute-start.19 = (bf16[640,128]{1,0:T(8,128)(2,1)S(1)}, bf16[640,128]{1,0:T(8,128)(2,1)S(1)}, u32[]{:S(2)}, u32[]{:S(2)}) collective-permute-start(bf16[640,128]{1,0:T(8,128)(2,1)S(1)} %get-tuple-element.86.old_right), channel_id=1, source_target_pairs={{0,2},{1,3},{2,4},{3,5},{4,6},{5,7},{6,8},{7,9},{8,10},{9,11},{10,... | collective-permute-start | bytes 491528 | tf_op jit(solution)/shard_map/ppermute | solution.py:266
  62.0 8.7 %collective-permute-start.23 = (bf16[640,128]{1,0:T(8,128)(2,1)S(1)}, bf16[640,128]{1,0:T(8,128)(2,1)S(1)}, u32[]{:S(2)}, u32[]{:S(2)}) collective-permute-start(bf16[640,128]{1,0:T(8,128)(2,1)S(1)} %shard_map.48), channel_id=1, source_target_pairs={{0,2},{1,3},{2,4},{3,5},{4,0},{5,1},{6,8},{7,9},{8,10},{9,11},{10,... | collective-permute-start | bytes 491528 | tf_op jit(solution)/shard_map/ppermute | solution.py:266
  62.9 10.7 %collective-permute-start.27 = (bf16[640,256]{1,0:T(8,128)(2,1)S(1)}, bf16[640,256]{1,0:T(8,128)(2,1)S(1)}, u32[]{:S(2)}, u32[]{:S(2)}) collective-permute-start(bf16[640,256]{1,0:T(8,128)(2,1)S(1)} %shard_map.54), channel_id=1, source_target_pairs={{0,16},{16,0},{1,17},{17,1},{2,18},{18,2},{3,19},{19,3},{4,20},{20... | collective-permute-start | bytes 983048 | tf_op jit(solution)/shard_map/ppermute | solution.py:269
  (4 other events, 20.2 us)
